TPU v7x, 128 devices: a whole 4x4x4 slice. The times are simulated.
128 devices in a mesh: gx: 8 (over z, core), gy: 4 (over y), gz: 4 (over x).
Axes of the slice: x: 4, y: 4, z: 4, core: 2. Of those that a mesh axis runs over, the one named last changes fastest.
Arguments:
- orbitals: bfloat16 [2, 512, 64000], P(None, ('gx', 'gy', 'gz')), may hold values from -6 to 6
- dest: int32 [512], replicated, may hold values from 0 to 127, as said below
- partners: int32 [512, 2], replicated, may hold values from 0 to 511, as said below
- anchors: int32 [512, 3], replicated, may hold values from 0 to 767, as said below
Outputs:
- exchange: float32 [2, 896, 64000], P(None, ('gx', 'gy', 'gz'))
Inputs may be any that keep to these rules, and one draw needn't show every extreme that they name: `dest`: box i goes to its first device or to the device just before or just after it in the numbering; a device passes at most 2 boxes to the device before and at most 1 to the device after, and holds at most 7 boxes after the move; every device holds one or more; each of these three bounds is reached in every draw. A box's partners (the box itself or the same box twice may occur) sit at first on the same device as the box or on one next to it in the numbering, and after the move likewise. Before the move and after it, exactly 1 of the boxes of a device are partners of boxes on the device after it, and exactly 1 are partners of boxes on the device before it (where that device exists). `anchors`: columns are the three grid dimensions, each within its own grid extent; along each, a partner's anchor differs from its box's by at most 20 cells, the difference taken modulo the grid.
All inputs are finite; a program needn't handle non-finite values.
Results may differ from a plain program's by a relative error of at most 0.0072.
Values may be sent and summed in bfloat16 or wider, within the bound.
A program may use at most 64 MiB of HBM per device.

v0:
```python
import jax
import jax.numpy as jnp
from jax import lax
from jax.sharding import PartitionSpec as P

EDGE = 40
PARTNERS = 2
GRID_X = 768
GRID_Y = 384
GRID_Z = 384
BOX_DEV = 4
BACK = 2
AHEAD = 1
CAP = 7


SCREEN = 0.001
FINEST = lax.Precision.HIGHEST


def from_behind(value, axis, steps):
    count = lax.axis_size(axis)
    initial, last = (max(0, -steps), min(count, count - steps))
    return lax.ppermute(value, axis, [(source, source + steps) for source in range(initial, last)])


def sine_basis(edge_cells):
    counter = jnp.arange(edge_cells, dtype=jnp.float32) + 1.0
    angles = jnp.pi * counter[:, None] * counter[None, :] / (edge_cells + 1.0)
    sine_table = (jnp.sqrt(2.0 / (edge_cells + 1.0)) * jnp.sin(angles)).astype(jnp.bfloat16)
    levels = 2.0 - 2.0 * jnp.cos(jnp.pi * counter / (edge_cells + 1.0))
    spectrum = levels[:, None, None] + levels[None, :, None] + levels[None, None, :] + SCREEN
    return (sine_table, spectrum)


def sine_pass(volume, sine_table):
    volume = jnp.einsum(
        "ak,psabc->pskbc", sine_table, volume, preferred_element_type=jnp.float32
    ).astype(jnp.bfloat16)
    volume = jnp.einsum(
        "bk,psabc->psakc", sine_table, volume, preferred_element_type=jnp.float32
    ).astype(jnp.bfloat16)
    return jnp.einsum("ck,psabc->psabk", sine_table, volume, preferred_element_type=jnp.float32)


def pair_sum(center, partner_boxes, deltas, sine_table, spectrum):
    spin_count = center.shape[0]
    edge_cells = sine_table.shape[0]
    cube_shape = (spin_count, edge_cells, edge_cells, edge_cells)
    center_cube = center.astype(jnp.float32).reshape(cube_shape)
    moving = partner_boxes.reshape((partner_boxes.shape[0],) + cube_shape)
    cell_line = jnp.arange(edge_cells, dtype=jnp.int32)
    shifters = [
        (
            cell_line[None, None, :]
            == cell_line[None, :, None] - deltas[:, dimension][:, None, None]
        ).astype(jnp.bfloat16)
        for dimension in range(3)
    ]
    moving = jnp.einsum(
        "pxa,psabc->psxbc", shifters[0], moving, preferred_element_type=jnp.float32
    ).astype(jnp.bfloat16)
    moving = jnp.einsum(
        "pyb,psxbc->psxyc", shifters[1], moving, preferred_element_type=jnp.float32
    ).astype(jnp.bfloat16)
    shifted = jnp.einsum(
        "pzc,psxyc->psxyz", shifters[2], moving, preferred_element_type=jnp.float32
    )
    density = (center_cube[None] * shifted).astype(jnp.bfloat16)
    spectral = (sine_pass(density, sine_table) / spectrum).astype(jnp.bfloat16)
    potential = sine_pass(spectral, sine_table)
    return jnp.sum(potential * shifted, axis=0).reshape(spin_count, -1)


def wrapped(difference):
    extent = jnp.array([GRID_X, GRID_Y, GRID_Z], jnp.int32)
    return (difference + extent // 2) % extent - extent // 2


def routing(dest, device):
    filler = jnp.full((2 * BOX_DEV,), -1, jnp.int32)
    padded = jnp.concatenate([filler, dest, filler])
    nearby = lax.dynamic_slice_in_dim(padded, device * BOX_DEV, 5 * BOX_DEV)
    window_pos = jnp.arange(5 * BOX_DEV, dtype=jnp.int32)
    blocks = window_pos // BOX_DEV
    earlier = (nearby[:, None] == nearby[None, :]) & (window_pos[None, :] < window_pos[:, None])
    rankings = jnp.sum(earlier.astype(jnp.int32), axis=1)
    inside = jnp.sum((earlier & (blocks[:, None] == blocks[None, :])).astype(jnp.int32), axis=1)
    return (nearby, rankings, inside)


def select_rows(wanted, inside, row_count):
    counter = jnp.arange(row_count, dtype=jnp.int32)
    return (wanted[None, :] & (inside[None, :] == counter[:, None])).astype(jnp.float32)


def arrival(match_part, inside_part, row_count):
    counter = jnp.arange(row_count, dtype=jnp.int32)
    picker = (inside_part[:, None] == counter[None, :]).astype(jnp.float32)
    return jnp.dot(match_part, picker, precision=FINEST)


def combine(placers, portions):
    summed = 0
    for placer, portion in zip(placers, portions):
        summed = summed + jnp.einsum(
            "ka,sac->skc", placer.astype(portion.dtype), portion, preferred_element_type=jnp.float32
        )
    return summed


def fetch_box(prev_boxes, self_boxes, next_boxes, side_code, row_index):
    from_prev = lax.dynamic_index_in_dim(prev_boxes, row_index, 1, keepdims=False)
    from_self = lax.dynamic_index_in_dim(self_boxes, row_index, 1, keepdims=False)
    from_next = lax.dynamic_index_in_dim(next_boxes, row_index, 1, keepdims=False)
    return jnp.where(side_code < 0, from_prev, jnp.where(side_code == 0, from_self, from_next))


def neighbour_rows(source, full_rows):
    prev_rows = from_behind(source, ("gx", "gy", "gz"), 1)
    next_rows = from_behind(source, ("gx", "gy", "gz"), -1)
    return (prev_rows, next_rows, full_rows, full_rows)


def shards(orbitals, dest, partners, anchors):
    device = lax.axis_index(("gx", "gy", "gz"))
    sine_table, spectrum = sine_basis(EDGE)
    nearby, rankings, inside = routing(dest, device)
    first_near = (device - 2) * BOX_DEV
    own_dest = nearby[2 * BOX_DEV : 3 * BOX_DEV]
    own_inside = inside[2 * BOX_DEV : 3 * BOX_DEV]
    pick_ahead = select_rows(own_dest == device + 1, own_inside, AHEAD)
    pick_back = select_rows(own_dest == device - 1, own_inside, BACK)
    slot_line = jnp.arange(CAP, dtype=jnp.int32)
    matches = (nearby[None, :] == device) & (rankings[None, :] == slot_line[:, None])
    match_values = matches.astype(jnp.float32)
    placers = (
        arrival(match_values[:, BOX_DEV : 2 * BOX_DEV], inside[BOX_DEV : 2 * BOX_DEV], AHEAD),
        match_values[:, 2 * BOX_DEV : 3 * BOX_DEV],
        arrival(
            match_values[:, 3 * BOX_DEV : 4 * BOX_DEV], inside[3 * BOX_DEV : 4 * BOX_DEV], BACK
        ),
    )
    total_boxes = dest.shape[0]
    ahead_boxes = jnp.einsum(
        "ar,src->sac", pick_ahead.astype(jnp.bfloat16), orbitals, preferred_element_type=jnp.float32
    ).astype(jnp.bfloat16)
    back_boxes = jnp.einsum(
        "ar,src->sac", pick_back.astype(jnp.bfloat16), orbitals, preferred_element_type=jnp.float32
    ).astype(jnp.bfloat16)
    arrived_prev = from_behind(ahead_boxes, ("gx", "gy", "gz"), 1)
    arrived_next = from_behind(back_boxes, ("gx", "gy", "gz"), -1)
    settled = combine(placers, (arrived_prev, orbitals, arrived_next)).astype(jnp.bfloat16)
    window_ids = first_near + jnp.arange(5 * BOX_DEV, dtype=jnp.int32)
    slot_box = jnp.sum(jnp.where(matches, window_ids[None, :], 0), axis=1)
    occupied = jnp.sum(match_values, axis=1)
    safe_box = jnp.clip(slot_box, 0, total_boxes - 1)
    partner_ids = jnp.take(partners, safe_box, axis=0)
    near_pos = jnp.clip(partner_ids - first_near, 0, 5 * BOX_DEV - 1)
    side_codes = jnp.take(nearby, near_pos) - device
    partner_slots = jnp.take(rankings, near_pos)
    deltas = wrapped(
        jnp.take(anchors, partner_ids, axis=0) - jnp.take(anchors, safe_box, axis=0)[:, None, :]
    )
    prev_slots, next_slots, prev_index, next_index = neighbour_rows(settled, partner_slots)
    row_pick = jnp.where(
        side_codes < 0, prev_index, jnp.where(side_codes == 0, partner_slots, next_index)
    )

    def one_slot(slot_items):
        slot_index, side_row, row_slots, delta_row = slot_items
        center = lax.dynamic_index_in_dim(settled, slot_index, 1, keepdims=False)
        partner_boxes = jnp.stack(
            [
                fetch_box(prev_slots, settled, next_slots, side_row[number], row_slots[number])
                for number in range(PARTNERS)
            ]
        )
        return pair_sum(center, partner_boxes, delta_row, sine_table, spectrum)

    box_terms = lax.map(one_slot, (slot_line, side_codes, row_pick, deltas))
    exchange = jnp.moveaxis(box_terms, 0, 1) * occupied[None, :, None]
    return exchange


def solution(mesh):
    return jax.shard_map(
        shards,
        mesh=mesh,
        in_specs=(P(None, ("gx", "gy", "gz"), None), P(), P(), P()),
        out_specs=P(None, ("gx", "gy", "gz"), None),
        check_vma=False,
    )
```

profile of v0, /device:TPU:96, one launch (start us, length us, event | category | flops | bytes accessed | tf_op | source)
XLA Modules:
  0.0 483.3 jit_solution(17301204732753911804)
XLA Ops:
  6.5 6.4 %collective-permute-start.1 = (bf16[2,2,64000]{2,1,0:T(2,128)(2,1)S(1)}, bf16[2,2,64000]{2,1,0:T(2,128)(2,1)S(1)}, u32[]{:S(2)}, u32[]{:S(2)}) collective-permute-start(bf16[2,2,64000]{2,1,0:T(2,128)(2,1)S(1)} %fusion.74), channel_id=1, source_target_pairs={{1,0},{2,1},{3,2},{4,3},{5,4},{6,5},{7,6},{8,7},{9,8},{10,9},{11,1... | collective-permute-start | bytes 1536008 | tf_op jit(solution)/shard_map/ppermute | solution.py:24
  19.4 4.2 collective-permute-done.1
  31.4 8.0 %collective-permute-start.3 = (bf16[2,7,64000]{2,0,1:T(2,128)(2,1)}, bf16[2,7,64000]{2,0,1:T(2,128)(2,1)}, u32[]{:S(2)}, u32[]{:S(2)}) collective-permute-start(bf16[2,7,64000]{2,0,1:T(2,128)(2,1)} %copy.95), channel_id=1, source_target_pairs={{1,0},{2,1},{3,2},{4,3},{5,4},{6,5},{7,6},{8,7},{9,8},{10,9},{11,1... | collective-permute-start | bytes 5376008 | tf_op jit(solution)/shard_map/ppermute | solution.py:24
  41.3 34.6 %collective-permute-done.2 = bf16[2,7,64000]{2,0,1:T(2,128)(2,1)} collective-permute-done((bf16[2,7,64000]{2,0,1:T(2,128)(2,1)}, bf16[2,7,64000]{2,0,1:T(2,128)(2,1)}, u32[]{:S(2)}, u32[]{:S(2)}) %collective-permute-start.2) | collective-permute-done | bytes 1792032 | tf_op jit(solution)/shard_map/ppermute | solution.py:24
  77.0 401.2 %while.12 = (s32[]{:T(128)}, f32[7,2,64000]{2,1,0:T(2,128)}, s32[7]{0:T(128)S(1)}, bf16[2,7,64000]{2,0,1:T(2,128)(2,1)}, s32[7,2]{1,0:T(8,128)S(1)}, /*index=5*/...) while((s32[]{:T(128)}, f32[7,2,64000]{2,1,0:T(2,128)}, ...), condition=%wide.region_5.7_spmd.clone.clone, body=%wide.region_3.6_spmd.clone.clone.sunk | while | flops 188336256 | bytes 24330844 | solution.py:181
  103.3 4.8 multiply_convert_fusion.3
  121.0 4.0 copy.138
  125.0 5.7 %multiply_reduce_fusion.2 = f32[2,40,40,40]{3,2,1,0:T(8,128)} fusion(f32[2,2,40,40,40]{4,3,2,1,0:T(8,128)} %get-tuple-element.370, bf16[2,2,40,40,40]{3,4,2,1,0:T(8,128)(2,1)S(1)} %copy.138, f32[40]{0:T(128)S(1)} %get-tuple-element.415, f32[40]{0:T(128)S(1)} %get-tuple-element.416), kind=kOutput, calls=%fused_computation.7.clone.1 | convolution fusion | flops 41612800 | bytes 2048320 | tf_op jit(solution)/shard_map/while/body/eval_jaxpr/ck,psabc->psabk/dot_general | solution.py:43
  160.6 4.8 multiply_convert_fusion.3
  178.3 4.0 copy.138
  182.4 5.7 %multiply_reduce_fusion.2 = f32[2,40,40,40]{3,2,1,0:T(8,128)} fusion(f32[2,2,40,40,40]{4,3,2,1,0:T(8,128)} %get-tuple-element.370, bf16[2,2,40,40,40]{3,4,2,1,0:T(8,128)(2,1)S(1)} %copy.138, f32[40]{0:T(128)S(1)} %get-tuple-element.415, f32[40]{0:T(128)S(1)} %get-tuple-element.416), kind=kOutput, calls=%fused_computation.7.clone.1 | convolution fusion | flops 41612800 | bytes 2048320 | tf_op jit(solution)/shard_map/while/body/eval_jaxpr/ck,psabc->psabk/dot_general | solution.py:43
  217.9 4.8 multiply_convert_fusion.3
  235.6 4.0 copy.138
  239.7 5.7 %multiply_reduce_fusion.2 = f32[2,40,40,40]{3,2,1,0:T(8,128)} fusion(f32[2,2,40,40,40]{4,3,2,1,0:T(8,128)} %get-tuple-element.370, bf16[2,2,40,40,40]{3,4,2,1,0:T(8,128)(2,1)S(1)} %copy.138, f32[40]{0:T(128)S(1)} %get-tuple-element.415, f32[40]{0:T(128)S(1)} %get-tuple-element.416), kind=kOutput, calls=%fused_computation.7.clone.1 | convolution fusion | flops 41612800 | bytes 2048320 | tf_op jit(solution)/shard_map/while/body/eval_jaxpr/ck,psabc->psabk/dot_general | solution.py:43
  275.2 4.8 multiply_convert_fusion.3
  297.0 5.7 %multiply_reduce_fusion.2 = f32[2,40,40,40]{3,2,1,0:T(8,128)} fusion(f32[2,2,40,40,40]{4,3,2,1,0:T(8,128)} %get-tuple-element.370, bf16[2,2,40,40,40]{3,4,2,1,0:T(8,128)(2,1)S(1)} %copy.138, f32[40]{0:T(128)S(1)} %get-tuple-element.415, f32[40]{0:T(128)S(1)} %get-tuple-element.416), kind=kOutput, calls=%fused_computation.7.clone.1 | convolution fusion | flops 41612800 | bytes 2048320 | tf_op jit(solution)/shard_map/while/body/eval_jaxpr/ck,psabc->psabk/dot_general | solution.py:43
  332.5 4.8 multiply_convert_fusion.3
  354.3 5.7 %multiply_reduce_fusion.2 = f32[2,40,40,40]{3,2,1,0:T(8,128)} fusion(f32[2,2,40,40,40]{4,3,2,1,0:T(8,128)} %get-tuple-element.370, bf16[2,2,40,40,40]{3,4,2,1,0:T(8,128)(2,1)S(1)} %copy.138, f32[40]{0:T(128)S(1)} %get-tuple-element.415, f32[40]{0:T(128)S(1)} %get-tuple-element.416), kind=kOutput, calls=%fused_computation.7.clone.1 | convolution fusion | flops 41612800 | bytes 2048320 | tf_op jit(solution)/shard_map/while/body/eval_jaxpr/ck,psabc->psabk/dot_general | solution.py:43
  389.8 4.8 multiply_convert_fusion.3
  411.6 5.7 %multiply_reduce_fusion.2 = f32[2,40,40,40]{3,2,1,0:T(8,128)} fusion(f32[2,2,40,40,40]{4,3,2,1,0:T(8,128)} %get-tuple-element.370, bf16[2,2,40,40,40]{3,4,2,1,0:T(8,128)(2,1)S(1)} %copy.138, f32[40]{0:T(128)S(1)} %get-tuple-element.415, f32[40]{0:T(128)S(1)} %get-tuple-element.416), kind=kOutput, calls=%fused_computation.7.clone.1 | convolution fusion | flops 41612800 | bytes 2048320 | tf_op jit(solution)/shard_map/while/body/eval_jaxpr/ck,psabc->psabk/dot_general | solution.py:43
  447.2 4.8 multiply_convert_fusion.3
  464.9 4.0 copy.138
  468.9 5.7 %multiply_reduce_fusion.2 = f32[2,40,40,40]{3,2,1,0:T(8,128)} fusion(f32[2,2,40,40,40]{4,3,2,1,0:T(8,128)} %get-tuple-element.370, bf16[2,2,40,40,40]{3,4,2,1,0:T(8,128)(2,1)S(1)} %copy.138, f32[40]{0:T(128)S(1)} %get-tuple-element.415, f32[40]{0:T(128)S(1)} %get-tuple-element.416), kind=kOutput, calls=%fused_computation.7.clone.1 | convolution fusion | flops 41612800 | bytes 2048320 | tf_op jit(solution)/shard_map/while/body/eval_jaxpr/ck,psabc->psabk/dot_general | solution.py:43
  478.1 5.1 %multiply_bitcast_fusion = f32[2,7,64000]{2,0,1:T(2,128)} fusion(f32[7,2,64000]{2,1,0:T(2,128)} %get-tuple-element.78, f32[7]{0:T(128)S(1)} %convert_reduce_fusion.2), kind=kLoop, calls=%fused_computation.84 | loop fusion | flops 896000 | bytes 7168028 | tf_op jit(solution)/shard_map/mul | solution.py:182
  (262 shorter events, 277.9 us)
Async XLA Ops:
  0.0 1.2 copy-start
  2.3 17.0 %collective-permute-start = (bf16[2,1,64000]{2,0,1:T(2,128)(2,1)S(1)}, bf16[2,1,64000]{2,0,1:T(2,128)(2,1)S(1)}, u32[]{:S(2)}, u32[]{:S(2)}) collective-permute-start(bf16[2,1,64000]{2,0,1:T(2,128)(2,1)S(1)} %bitcast.193), channel_id=1, source_target_pairs={{0,1},{1,2},{2,3},{3,4},{4,5},{5,6},{6,7},{7,8},{8,9},{9,10},{10,1... | collective-permute-start | bytes 768008 | tf_op jit(solution)/shard_map/ppermute | solution.py:24
  6.5 17.1 %collective-permute-start.1 = (bf16[2,2,64000]{2,1,0:T(2,128)(2,1)S(1)}, bf16[2,2,64000]{2,1,0:T(2,128)(2,1)S(1)}, u32[]{:S(2)}, u32[]{:S(2)}) collective-permute-start(bf16[2,2,64000]{2,1,0:T(2,128)(2,1)S(1)} %fusion.74), channel_id=1, source_target_pairs={{1,0},{2,1},{3,2},{4,3},{5,4},{6,5},{7,6},{8,7},{9,8},{10,9},{11,1... | collective-permute-start | bytes 1536008 | tf_op jit(solution)/shard_map/ppermute | solution.py:24
  13.1 2.4 copy-start.4
  17.4 0.9 copy-start.3
  26.7 13.7 %copy-start.5 = (s32[3]{0:T(128)S(1)}, s32[3]{0:T(128)}, u32[]{:S(2)}) copy-start(s32[3]{0:T(128)} %constant.196) | copy-start | bytes 40
  26.8 13.7 %copy-start.6 = (s32[3]{0:T(128)S(1)}, s32[3]{0:T(128)}, u32[]{:S(2)}) copy-start(s32[3]{0:T(128)} %constant.198) | copy-start | bytes 40
  26.8 13.7 %copy-start.7 = (s32[3]{0:T(128)S(1)}, s32[3]{0:T(128)}, u32[]{:S(2)}) copy-start(s32[3]{0:T(128)} %constant.201) | copy-start | bytes 40
  29.5 46.4 %collective-permute-start.2 = (bf16[2,7,64000]{2,0,1:T(2,128)(2,1)}, bf16[2,7,64000]{2,0,1:T(2,128)(2,1)}, u32[]{:S(2)}, u32[]{:S(2)}) collective-permute-start(bf16[2,7,64000]{2,0,1:T(2,128)(2,1)} %copy.95), channel_id=1, source_target_pairs={{0,1},{1,2},{2,3},{3,4},{4,5},{5,6},{6,7},{7,8},{8,9},{9,10},{10,1... | collective-permute-start | bytes 5376008 | tf_op jit(solution)/shard_map/ppermute | solution.py:24
  31.4 45.6 %collective-permute-start.3 = (bf16[2,7,64000]{2,0,1:T(2,128)(2,1)}, bf16[2,7,64000]{2,0,1:T(2,128)(2,1)}, u32[]{:S(2)}, u32[]{:S(2)}) collective-permute-start(bf16[2,7,64000]{2,0,1:T(2,128)(2,1)} %copy.95), channel_id=1, source_target_pairs={{1,0},{2,1},{3,2},{4,3},{5,4},{6,5},{7,6},{8,7},{9,8},{10,9},{11,1... | collective-permute-start | bytes 5376008 | tf_op jit(solution)/shard_map/ppermute | solution.py:24
  96.8 3.7 copy-start.2
  100.5 2.8 copy-start.1
  154.1 3.7 copy-start.2
  157.8 2.8 copy-start.1
  211.5 3.7 copy-start.2
  215.1 2.8 copy-start.1
  268.8 3.7 copy-start.2
  272.4 2.8 copy-start.1
  326.1 3.7 copy-start.2
  329.8 2.8 copy-start.1
  383.4 3.7 copy-start.2
  387.1 2.8 copy-start.1
  440.7 3.7 copy-start.2
  444.4 2.8 copy-start.1
where the time goes:
time: 488 us; the launch traced here: 483 us
  local copies, waits for them, and re-layouts  176 us (36%)
  matrix products  157 us (32%)
  loops' own time  57.5 us (12%)
  waiting for transfers between devices  39.9 us (8%)
  other arithmetic  33 us (7%)
  starting transfers between devices  19.7 us (4%)
    dot_general x14, matrix products, sine_pass(): jnp.einsum('ck,psabc->psabk', sine_table, volume, preferred_element_type=...  66.6 us
    another operation x1, loops' own time, shards(): box_terms = lax.map(one_slot, (slot_line, side_codes, row_pick, deltas))  57.5 us
    convert_element_type x14, local copies, waits for them, and re-layouts, sine_pass(): volume = jnp.einsum('ak,psabc->pskbc', sine_table, volume, preferred_elem...  53.7 us
    ppermute x4, waiting for transfers between devices, from_behind(): lax.ppermute(value, axis, [(source, source + steps) for source in range(i...  39.9 us
    dot_general x14, matrix products, sine_pass(): jnp.einsum('ak,psabc->pskbc', sine_table, volume, preferred_element_type=...  36.3 us
    dot_general x7, matrix products, pair_sum(): jnp.einsum('pzc,psxyc->psxyz', shifters[2], moving, preferred_element_typ...  33.5 us
    select_n x28, local copies, waits for them, and re-layouts, fetch_box(): jnp.where(side_code < 0, from_prev, jnp.where(side_code == 0, from_self,...  31.1 us
    convert_element_type x7, local copies, waits for them, and re-layouts, pair_sum(): moving = jnp.einsum('pxa,psabc->psxbc', shifters[0], moving, preferred_el...  25.6 us
  transfers between devices with their start and end apart: 4, of which 3 were waited for; matrix products, arithmetic and copies ran while one was open for 2% of the time, Pallas kernels for 0%

commit v1 on v0

v1 whole, which is shorter than its diff:
```python
import functools

import jax
import jax.numpy as jnp
import ml_dtypes
import numpy as np
from jax import lax
from jax.experimental import pallas as pl
from jax.experimental.pallas import tpu as pltpu
from jax.sharding import PartitionSpec as P

AXES = ("gx", "gy", "gz")
DEVICES = 128
SPINS = 2
EDGE = 40
PLANE = EDGE * EDGE
CELLS = EDGE * PLANE
GRID = (768, 384, 384)
BOX_DEV = 4
CAP = 7
SCREEN = 0.001

LANE = 128
TILES = 13
WIDTH = TILES * LANE
OFF = (WIDTH - PLANE) // 2
MARGIN = 7 * LANE
WIDE = WIDTH + 2 * MARGIN
ROWS = SPINS * EDGE
TOP = 24
PAIR_ROWS = BOX_DEV * 2 * ROWS


def tables():
    counter = np.arange(EDGE, dtype=np.float64) + 1.0
    angles = np.pi * counter[:, None] * counter[None, :] / (EDGE + 1.0)
    sine = (np.sqrt(2.0 / (EDGE + 1.0)) * np.sin(angles)).astype(ml_dtypes.bfloat16)
    levels = 2.0 - 2.0 * np.cos(np.pi * counter / (EDGE + 1.0))
    plane = (levels[:, None] + levels[None, :]).reshape(-1)
    inverse = np.zeros((EDGE, WIDTH), np.float32)
    inverse[:, OFF : OFF + PLANE] = 1.0 / (levels[:, None] + plane[None, :] + SCREEN)
    inverse = np.concatenate([inverse, inverse], axis=0)
    sine32 = sine.astype(np.float32)
    first = np.kron(np.eye(4, dtype=np.float32), sine32).astype(ml_dtypes.bfloat16)
    both = np.zeros((WIDTH, WIDTH), np.float32)
    both[OFF : OFF + PLANE, OFF : OFF + PLANE] = np.kron(sine32, sine32)
    both = both.astype(ml_dtypes.bfloat16)
    cells = np.full((2, WIDTH), -1000, np.int32)
    cells[0, OFF : OFF + PLANE] = np.arange(PLANE) // EDGE
    cells[1, OFF : OFF + PLANE] = np.arange(PLANE) % EDGE
    return first, both, inverse, cells


def device_number():
    index = lax.axis_index(AXES[0])
    for name in AXES[1:]:
        index = index * lax.axis_size(name) + lax.axis_index(name)
    return index


def count(dest, first_box, device):
    total = 0
    for number in range(BOX_DEV):
        total = total + (dest[first_box + number] == device).astype(jnp.int32)
    return total


def position(backs, aheads, rank):
    place = backs + rank
    return place + jnp.where((place >= 2) & (aheads > 0), 1, 0)


def boxes_by_position(dest, device):
    base = device * BOX_DEV
    backs = count(dest, base, device - 1)
    aheads = count(dest, base, device + 1)
    order = [0] * BOX_DEV
    back_rank = stay_rank = 0
    for number in range(BOX_DEV):
        goal = dest[base + number]
        back = goal < device
        ahead = goal > device
        place = jnp.where(back, back_rank, jnp.where(ahead, 2, position(backs, aheads, stay_rank)))
        back_rank = back_rank + back.astype(jnp.int32)
        stay_rank = stay_rank + (goal == device).astype(jnp.int32)
        for spot in range(BOX_DEV):
            order[spot] = order[spot] + jnp.where(place == spot, number, 0)
    return order


def slot_sources(dest, device):
    base = device * BOX_DEV
    last = DEVICES - 1
    backs = count(dest, base, device - 1)
    aheads = count(dest, base, device + 1)
    stays = BOX_DEV - backs - aheads
    behind = jnp.maximum(device - 1, 0) * BOX_DEV
    front = jnp.minimum(device + 1, last) * BOX_DEV
    from_prev = jnp.where(device > 0, count(dest, behind, device), 0)
    from_next = jnp.where(device < last, count(dest, front, device), 0)
    sources = []
    for slot in range(CAP):
        rank = slot - from_prev
        late = rank - stays
        sources.append(
            jnp.where(
                rank < 0,
                4,
                jnp.where(
                    late < 0,
                    position(backs, aheads, rank),
                    jnp.where(late < from_next, 5 + late, 7),
                ),
            )
        )
    return sources


def shared_box(partners, device, other):
    inside = jnp.clip(other, 0, DEVICES - 1) * BOX_DEV
    chosen = 0
    for number in range(BOX_DEV):
        for which in range(2):
            partner = partners[which, inside + number] - device * BOX_DEV
            chosen = jnp.where((partner >= 0) & (partner < BOX_DEV), partner, chosen)
    return chosen


def wrapped(difference, extent):
    half = difference + extent // 2
    half = jnp.where(half < 0, half + extent, half)
    half = jnp.where(half >= extent, half - extent, half)
    return half - extent // 2


def unpack_rows(orbitals, store):
    def pair(number, carry):
        start = pl.multiple_of(number * 2 * PLANE, LANE)
        for spin in range(SPINS):
            cells = orbitals[spin, :, pl.ds(start, 2 * PLANE)].astype(jnp.float32)
            even = pltpu.roll(cells[:, :WIDTH], OFF, 1)
            odd = pltpu.roll(cells[:, 2 * PLANE - WIDTH :], WIDTH - OFF, 1)
            store(spin * EDGE + 2 * number, even)
            store(spin * EDGE + 2 * number + 1, odd)
        return carry

    lax.fori_loop(0, EDGE // 2, pair, 0)


def shift_pair(boxes, moved, density, cells, center_row, partner_row, delta, pair_row):
    flat = MARGIN - (delta[1] * EDGE + delta[2])
    column = flat // LANE
    turn = flat - column * LANE
    center_row = pl.multiple_of(center_row, 8)
    lanes = lax.broadcasted_iota(jnp.int32, (EDGE, LANE), 1)
    keep = lanes < LANE - turn
    rows = lax.broadcasted_iota(jnp.int32, (EDGE, LANE), 0) - delta[0]
    row_ok = (rows >= 0) & (rows < EDGE)

    def load(tile, spin):
        value = boxes[column + tile, pl.ds(partner_row + spin * EDGE - delta[0], EDGE), :]
        return pltpu.roll(value, LANE - turn, 1)

    before = [load(0, spin) for spin in range(SPINS)]
    for tile in range(TILES):
        span = slice(tile * LANE, (tile + 1) * LANE)
        second = cells[0:1, span] - delta[1]
        third = cells[1:2, span] - delta[2]
        inside = (second >= 0) & (second < EDGE) & (third >= 0) & (third < EDGE)
        inside = inside & (cells[0:1, span] >= 0)
        ok = row_ok & inside
        after = [load(tile + 1, spin) for spin in range(SPINS)]
        values = []
        products = []
        for spin in range(SPINS):
            value = jnp.where(ok, jnp.where(keep, before[spin], after[spin]), 0.0)
            center = boxes[MARGIN // LANE + tile, pl.ds(center_row + spin * EDGE, EDGE), :]
            values.append(value)
            products.append(center * value)
        before = after
        target = pl.ds(pl.multiple_of(pair_row, ROWS), ROWS)
        moved[target, span] = jnp.concatenate(values, axis=0)
        density[target, span] = jnp.concatenate(products, axis=0).astype(jnp.bfloat16)


CHUNKS = [(start, min(256, WIDTH - start)) for start in range(0, WIDTH, 256)]


def solve(density, work, first, both, inverse):
    rows = density.shape[0]
    for block in range(rows // (2 * ROWS)):
        span = slice(block * 2 * ROWS, (block + 1) * 2 * ROWS)
        work[span, :] = jnp.dot(
            first[...], density[span, :], preferred_element_type=jnp.float32
        ).astype(jnp.bfloat16)
    for start, size in CHUNKS:
        scale = inverse[:, start : start + size]
        out = jnp.dot(work[...], both[:, start : start + size], preferred_element_type=jnp.float32)
        out = out.reshape(rows // ROWS, ROWS, size) * scale[None]
        density[:, start : start + size] = out.reshape(rows, size).astype(jnp.bfloat16)
    for start, size in CHUNKS:
        work[:, start : start + size] = jnp.dot(
            density[...], both[:, start : start + size], preferred_element_type=jnp.float32
        ).astype(jnp.bfloat16)


def pack_kernel(dest, partners, orbitals, rows, to_next, to_prev, scratch):
    device = device_number()

    def store(row, value):
        for tile in range(TILES):
            scratch[tile, pl.ds(row, BOX_DEV, stride=ROWS), :] = value[:, tile * LANE : (tile + 1) * LANE]

    unpack_rows(orbitals, store)
    rows[...] = scratch[...].astype(jnp.bfloat16)
    ahead = shared_box(partners, device, device + 1)
    back = shared_box(partners, device, device - 1)
    to_next[...] = scratch[:, pl.ds(pl.multiple_of(ahead * ROWS, 8), ROWS), :].astype(jnp.bfloat16)
    to_prev[...] = scratch[:, pl.ds(pl.multiple_of(back * ROWS, 8), ROWS), :].astype(jnp.bfloat16)


def solve_kernel(
    dest, partners, anchors, rows, prev_box, next_box, first, both, inverse, cells,
    results, sends, boxes, moved, density, work,
):
    device = device_number()
    own = BOX_DEV * ROWS
    middle = slice(MARGIN // LANE, MARGIN // LANE + TILES)
    boxes[middle, TOP : TOP + own, :] = rows[...].astype(jnp.float32)
    boxes[middle, TOP + own : TOP + own + ROWS, :] = prev_box[...].astype(jnp.float32)
    boxes[middle, TOP + own + ROWS : TOP + own + 2 * ROWS, :] = next_box[...].astype(jnp.float32)
    order = boxes_by_position(dest, device)
    base = device * BOX_DEV
    for spot in range(BOX_DEV):
        box = base + order[spot]
        for which in range(2):
            partner = partners[which, box]
            local = partner - base
            place = jnp.where(local < 0, 4, jnp.where(local >= BOX_DEV, 5, local))
            delta = [
                wrapped(anchors[dim, partner] - anchors[dim, box], GRID[dim]) for dim in range(3)
            ]
            shift_pair(
                boxes, moved, density, cells, TOP + order[spot] * ROWS, TOP + place * ROWS, delta,
                (spot * 2 + which) * ROWS,
            )
    solve(density, work, first, both, inverse)
    for spot in range(BOX_DEV):
        span = slice(spot * 2 * ROWS, (spot + 1) * 2 * ROWS)
        potential = jnp.dot(first[...], work[span, :], preferred_element_type=jnp.float32)
        terms = potential * moved[span, :]
        total = terms[:ROWS] + terms[ROWS:]
        for tile in range(TILES):
            part = total[:, tile * LANE : (tile + 1) * LANE]
            results[tile, spot * ROWS : (spot + 1) * ROWS, :] = part
            if spot < 3:
                sends[spot, tile, :, :] = part.astype(jnp.bfloat16)


def assemble_kernel(dest, results, prev_results, next_results, out, scratch):
    device = device_number()
    slot = pl.program_id(0)

    @pl.when(slot == 0)
    def _():
        scratch[:, : 4 * ROWS, :] = results[...]
        scratch[:, 4 * ROWS : 5 * ROWS, :] = prev_results[0].astype(jnp.float32)
        scratch[:, 5 * ROWS : 6 * ROWS, :] = next_results[0].astype(jnp.float32)
        scratch[:, 6 * ROWS : 7 * ROWS, :] = next_results[1].astype(jnp.float32)
        scratch[:, 7 * ROWS :, :] = jnp.zeros((TILES, ROWS, LANE), jnp.float32)

    sources = slot_sources(dest, device)
    source = sources[0]
    for number in range(1, CAP):
        source = jnp.where(slot == number, sources[number], source)
    lanes = lax.broadcasted_iota(jnp.int32, (SPINS, LANE), 1)

    def line(row):
        pieces = [scratch[tile, pl.ds(row, SPINS, stride=EDGE), :] for tile in range(TILES)]
        return jnp.concatenate(pieces, axis=1)

    def pair(number, carry):
        row = source * ROWS + 2 * number
        even = pltpu.roll(line(row), WIDTH - OFF, 1)
        odd = pltpu.roll(line(row + 1), OFF, 1)
        middle = jnp.where(lanes < LANE // 2, even[:, WIDTH - LANE :], odd[:, :LANE])
        start = pl.multiple_of(number * 2 * PLANE, LANE)
        cells = jnp.concatenate([even[:, : WIDTH - LANE], middle, odd[:, LANE:]], axis=1)
        out[0, :, pl.ds(start, 2 * PLANE)] = cells
        return carry

    lax.fori_loop(0, EDGE // 2, pair, 0)


VMEM_LIMIT = 56 * 1024 * 1024


def shards(orbitals, dest, partners, anchors):
    first, both, inverse, cells = (jnp.asarray(table) for table in tables())
    partners = partners.T
    anchors = anchors.T
    smem = pl.BlockSpec(memory_space=pltpu.SMEM)
    vmem = pl.BlockSpec(memory_space=pltpu.VMEM)
    params = pltpu.CompilerParams(vmem_limit_bytes=VMEM_LIMIT)
    own = BOX_DEV * ROWS
    box_shape = jax.ShapeDtypeStruct((TILES, ROWS, LANE), jnp.bfloat16)
    rows, to_next, to_prev = pl.pallas_call(
        pack_kernel,
        out_shape=(jax.ShapeDtypeStruct((TILES, own, LANE), jnp.bfloat16), box_shape, box_shape),
        in_specs=[smem, smem, vmem],
        out_specs=[vmem] * 3,
        scratch_shapes=[pltpu.VMEM((TILES, own, LANE), jnp.float32)],
        compiler_params=params,
    )(dest, partners, orbitals)
    ahead = [(number, number + 1) for number in range(DEVICES - 1)]
    back = [(number + 1, number) for number in range(DEVICES - 1)]
    prev_box = lax.ppermute(to_next, AXES, ahead)
    next_box = lax.ppermute(to_prev, AXES, back)
    results, sends = pl.pallas_call(
        solve_kernel,
        out_shape=(
            jax.ShapeDtypeStruct((TILES, own, LANE), jnp.float32),
            jax.ShapeDtypeStruct((3, TILES, ROWS, LANE), jnp.bfloat16),
        ),
        in_specs=[smem] * 3 + [vmem] * 7,
        out_specs=[vmem] * 2,
        scratch_shapes=[
            pltpu.VMEM((WIDE // LANE, TOP + 6 * ROWS + TOP, LANE), jnp.float32),
            pltpu.VMEM((PAIR_ROWS, WIDTH), jnp.float32),
            pltpu.VMEM((PAIR_ROWS, WIDTH), jnp.bfloat16),
            pltpu.VMEM((PAIR_ROWS, WIDTH), jnp.bfloat16),
        ],
        compiler_params=params,
    )(dest, partners, anchors, rows, prev_box, next_box, first, both, inverse, cells)
    prev_results = lax.ppermute(sends[2:], AXES, ahead)
    next_results = lax.ppermute(sends[:2], AXES, back)
    out = pl.pallas_call(
        assemble_kernel,
        out_shape=jax.ShapeDtypeStruct((CAP, SPINS, CELLS), jnp.float32),
        grid=(CAP,),
        in_specs=[smem, vmem, vmem, vmem],
        out_specs=pl.BlockSpec((1, SPINS, CELLS), lambda slot: (slot, 0, 0)),
        scratch_shapes=[pltpu.VMEM((TILES, 8 * ROWS, LANE), jnp.float32)],
        compiler_params=params,
    )(dest, results, prev_results, next_results)
    return jnp.transpose(out, (1, 0, 2))


def solution(mesh):
    return jax.shard_map(
        shards,
        mesh=mesh,
        in_specs=(P(None, AXES, None), P(), P(), P()),
        out_specs=P(None, AXES, None),
        check_vma=False,
    )
```

time: 488 us -> 77.9 us (0.16)
  local copies, waits for them, and re-layouts: 176 us -> 3.65 us
  matrix products: 157 us -> 0 us
  loops' own time: 57.5 us -> 0 us
  Pallas kernels: 0 us -> 38.1 us
  other arithmetic: 33 us -> 0 us
  waiting for transfers between devices: 39.9 us -> 16.2 us
    dot_general x48 -> x0, matrix products: 157 us -> none  [the longest x14 66.6 us: sine_pass(): jnp.einsum('ck,psabc->psabk', sine_table, volume, preferred_element_type=...]
    convert_element_type x28 -> x0, local copies, waits for them, and re-layouts: 98.2 us -> none  [the longest x14 53.7 us: sine_pass(): volume = jnp.einsum('ak,psabc->pskbc', sine_table, volume, preferred_elem...]
    another operation x1 -> x0, loops' own time: 57.5 us -> none  [shards(): box_terms = lax.map(one_slot, (slot_line, side_codes, row_pick, deltas))]
    pallas_call x0 -> x3, Pallas kernels: none -> 38.1 us  [the longest x1 17.4 us: shards(): pl.pallas_call(assemble_kernel, out_shape=jax.ShapeDtypeStruct((CAP, SPIN...]
    select_n x31 -> x0, local copies, waits for them, and re-layouts: 31.3 us -> none  [the longest x28 31.1 us: fetch_box(): jnp.where(side_code < 0, from_prev, jnp.where(side_code == 0, from_self,...]
    ppermute x4, waiting for transfers between devices: 39.9 us -> 16.2 us  [the longest x1 10.4 us: shards(): prev_results = lax.ppermute(sends[2:], AXES, ahead)]
    select_n x13 -> x0, other arithmetic: 22.9 us -> none  [the longest x7 22.6 us: fetch_box(): jnp.where(side_code < 0, from_prev, jnp.where(side_code == 0, from_self,...]
    broadcast_in_dim x8 -> x0, local copies, waits for them, and re-layouts: 19.1 us -> none  [the longest x7 19 us: shards(): box_terms = lax.map(one_slot, (slot_line, side_codes, row_pick, deltas))]
  transfers between devices with their start and end apart: 4 -> 4, of which waited for: 3 -> 3; matrix products, arithmetic and copies ran while one was open for 2% -> 1% of each run, Pallas kernels for 0% -> 0%
where the time goes in v1:
time: 77.9 us; the launch traced here: 77.6 us
  Pallas kernels  38.1 us (49%)
  starting transfers between devices  19.6 us (25%)
  waiting for transfers between devices  16.2 us (21%)
  local copies, waits for them, and re-layouts  3.65 us (5%)
    pallas_call x1, Pallas kernels, shards(): pl.pallas_call(assemble_kernel, out_shape=jax.ShapeDtypeStruct((CAP, SPIN...  17.4 us
    pallas_call x1, Pallas kernels, shards(): pl.pallas_call(solve_kernel, out_shape=(jax.ShapeDtypeStruct((TILES, own,...  15.8 us
    ppermute x1, waiting for transfers between devices, shards(): prev_results = lax.ppermute(sends[2:], AXES, ahead)  10.4 us
    ppermute x1, starting transfers between devices, shards(): next_results = lax.ppermute(sends[:2], AXES, back)  7.94 us
    ppermute x1, starting transfers between devices, shards(): next_box = lax.ppermute(to_prev, AXES, back)  6.38 us
    pallas_call x1, Pallas kernels, shards(): pl.pallas_call(pack_kernel, out_shape=(jax.ShapeDtypeStruct((TILES, own,...  4.86 us
    ppermute x1, waiting for transfers between devices, shards(): prev_box = lax.ppermute(to_next, AXES, ahead)  4.61 us
    ppermute x1, starting transfers between devices, shards(): prev_box = lax.ppermute(to_next, AXES, ahead)  3.39 us
  transfers between devices with their start and end apart: 4, of which 3 were waited for; matrix products, arithmetic and copies ran while one was open for 1% of the time, Pallas kernels for 0%

profile of v1, /device:TPU:96, one launch (start us, length us, event | category | flops | bytes accessed | tf_op | source)
XLA Modules:
  0.0 77.6 jit_solution(13237362687739004358)
XLA Ops:
  0.0 4.9 %shard_map.82 = (bf16[13,320,128]{2,1,0:T(8,128)(2,1)}, bf16[13,80,128]{2,1,0:T(8,128)(2,1)}, bf16[13,80,128]{2,1,0:T(8,128)(2,1)}) custom-call(s32[512]{0:T(512)} %dest.5, s32[2,512]{1,0:T(2,128)} %bitcast.3, bf16[2,4,64000]{2,1,0:T(4,128)(2,1)} %orbitals.1), custom_call_target="tpu_custom_call" | custom-call | tf_op jit(solution)/shard_map/pallas_call | solution.py:307
  4.9 3.4 %collective-permute-start = (bf16[13,80,128]{2,1,0:T(8,128)(2,1)}, bf16[13,80,128]{2,1,0:T(8,128)(2,1)S(1)}, u32[]{:S(2)}, u32[]{:S(2)}) collective-permute-start(bf16[13,80,128]{2,1,0:T(8,128)(2,1)} %get-tuple-element.11), channel_id=1, source_target_pairs={{0,1},{1,2},{2,3},{3,4},{4,5},{5,6},{6,7},{7,8},{8,9},{9,10},{10,1... | collective-permute-start | bytes 798728 | tf_op jit(solution)/shard_map/ppermute | solution.py:317
  8.3 6.4 %collective-permute-start.1 = (bf16[13,80,128]{2,1,0:T(8,128)(2,1)}, bf16[13,80,128]{2,1,0:T(8,128)(2,1)S(1)}, u32[]{:S(2)}, u32[]{:S(2)}) collective-permute-start(bf16[13,80,128]{2,1,0:T(8,128)(2,1)} %get-tuple-element.12), channel_id=1, source_target_pairs={{1,0},{2,1},{3,2},{4,3},{5,4},{6,5},{7,6},{8,7},{9,8},{10,9},{11,1... | collective-permute-start | bytes 798728 | tf_op jit(solution)/shard_map/ppermute | solution.py:318
  14.6 4.6 %collective-permute-done.prev_box = bf16[13,80,128]{2,1,0:T(8,128)(2,1)S(1)} collective-permute-done((bf16[13,80,128]{2,1,0:T(8,128)(2,1)}, bf16[13,80,128]{2,1,0:T(8,128)(2,1)S(1)}, u32[]{:S(2)}, u32[]{:S(2)}) %collective-permute-start) | collective-permute-done | bytes 266272 | tf_op jit(solution)/shard_map/ppermute | solution.py:317
  19.3 0.0 copy-start.1
  19.3 1.1 %collective-permute-done.1.next_box = bf16[13,80,128]{2,1,0:T(8,128)(2,1)S(1)} collective-permute-done((bf16[13,80,128]{2,1,0:T(8,128)(2,1)}, bf16[13,80,128]{2,1,0:T(8,128)(2,1)S(1)}, u32[]{:S(2)}, u32[]{:S(2)}) %collective-permute-start.1) | collective-permute-done | bytes 266272 | tf_op jit(solution)/shard_map/ppermute | solution.py:318
  20.4 0.0 copy-start.2
  20.4 0.0 copy-done.1
  20.4 0.7 copy-done.2
  21.1 15.8 %shard_map.83 = (f32[13,320,128]{2,1,0:T(8,128)}, bf16[3,13,80,128]{3,2,1,0:T(8,128)(2,1)}) custom-call(s32[512]{0:T(512)} %dest.5, s32[2,512]{1,0:T(2,128)} %bitcast.4, s32[3,512]{1,0:T(4,128)} %bitcast.5, bf16[13,320,128]{2,1,0:T(8,128)(2,1)} %get-tuple-element.10.rows, bf16[13,80,128]{2,1,0:T(8,128)(2,1)} %copy-done.1, bf16[13,80,128]{2,1,0:T(8,128)(2,1)} %copy-done.2, ...), custom_call_target="tpu_custom_call" | custom-call | tf_op jit(solution)/shard_map/pallas_call | solution.py:319
  36.9 1.1 %slice.7 = bf16[2,13,80,128]{3,2,1,0:T(8,128)(2,1)S(1)} slice(bf16[3,13,80,128]{3,2,1,0:T(8,128)(2,1)} %get-tuple-element.14), slice={[0:2], [0:13], [0:80], [0:128]} | slice | bytes 1064960 | tf_op jit(solution)/shard_map/slice | solution.py:336
  38.0 7.9 %collective-permute-start.3 = (bf16[2,13,80,128]{3,2,1,0:T(8,128)(2,1)S(1)}, bf16[2,13,80,128]{3,2,1,0:T(8,128)(2,1)S(1)}, u32[]{:S(2)}, u32[]{:S(2)}) collective-permute-start(bf16[2,13,80,128]{3,2,1,0:T(8,128)(2,1)S(1)} %slice.7), channel_id=1, source_target_pairs={{1,0},{2,1},{3,2},{4,3},{5,4},{6,5},{7,6},{8,7},{9,8},{10,9},{11,1... | collective-permute-start | bytes 1597448 | tf_op jit(solution)/shard_map/ppermute | solution.py:336
  46.0 1.0 %slice.6 = bf16[1,13,80,128]{3,2,1,0:T(8,128)(2,1)S(1)} slice(bf16[3,13,80,128]{3,2,1,0:T(8,128)(2,1)} %get-tuple-element.14), slice={[2:3], [0:13], [0:80], [0:128]} | slice | bytes 532480 | tf_op jit(solution)/shard_map/slice | solution.py:335
  46.9 1.9 %collective-permute-start.2 = (bf16[1,13,80,128]{3,2,1,0:T(8,128)(2,1)S(1)}, bf16[1,13,80,128]{3,2,1,0:T(8,128)(2,1)S(1)}, u32[]{:S(2)}, u32[]{:S(2)}) collective-permute-start(bf16[1,13,80,128]{3,2,1,0:T(8,128)(2,1)S(1)} %slice.6), channel_id=1, source_target_pairs={{0,1},{1,2},{2,3},{3,4},{4,5},{5,6},{6,7},{7,8},{8,9},{9,10},{10,1... | collective-permute-start | bytes 798728 | tf_op jit(solution)/shard_map/ppermute | solution.py:335
  48.9 10.4 %collective-permute-done.2.prev_results = bf16[1,13,80,128]{3,2,1,0:T(8,128)(2,1)S(1)} collective-permute-done((bf16[1,13,80,128]{3,2,1,0:T(8,128)(2,1)S(1)}, bf16[1,13,80,128]{3,2,1,0:T(8,128)(2,1)S(1)}, u32[]{:S(2)}, u32[]{:S(2)}) %collective-permute-start.2) | collective-permute-done | bytes 266272 | tf_op jit(solution)/shard_map/ppermute | solution.py:335
  59.3 0.0 copy-start.3
  59.3 0.0 collective-permute-done.3.next_results
  59.3 0.0 copy-start
  59.3 0.7 copy-done.3
  60.0 0.2 copy-done
  60.2 17.4 %shard_map.84 = f32[7,2,64000]{2,1,0:T(2,128)} custom-call(s32[512]{0:T(512)} %dest.5, f32[13,320,128]{2,1,0:T(8,128)} %get-tuple-element.13.results, bf16[1,13,80,128]{3,2,1,0:T(8,128)(2,1)} %copy-done.3, bf16[2,13,80,128]{3,2,1,0:T(8,128)(2,1)} %copy-done), custom_call_target="tpu_custom_call" | custom-call | tf_op jit(solution)/shard_map/pallas_call | solution.py:337
Async XLA Ops:
  4.9 14.4 %collective-permute-start = (bf16[13,80,128]{2,1,0:T(8,128)(2,1)}, bf16[13,80,128]{2,1,0:T(8,128)(2,1)S(1)}, u32[]{:S(2)}, u32[]{:S(2)}) collective-permute-start(bf16[13,80,128]{2,1,0:T(8,128)(2,1)} %get-tuple-element.11), channel_id=1, source_target_pairs={{0,1},{1,2},{2,3},{3,4},{4,5},{5,6},{6,7},{7,8},{8,9},{9,10},{10,1... | collective-permute-start | bytes 798728 | tf_op jit(solution)/shard_map/ppermute | solution.py:317
  8.3 12.2 %collective-permute-start.1 = (bf16[13,80,128]{2,1,0:T(8,128)(2,1)}, bf16[13,80,128]{2,1,0:T(8,128)(2,1)S(1)}, u32[]{:S(2)}, u32[]{:S(2)}) collective-permute-start(bf16[13,80,128]{2,1,0:T(8,128)(2,1)} %get-tuple-element.12), channel_id=1, source_target_pairs={{1,0},{2,1},{3,2},{4,3},{5,4},{6,5},{7,6},{8,7},{9,8},{10,9},{11,1... | collective-permute-start | bytes 798728 | tf_op jit(solution)/shard_map/ppermute | solution.py:318
  19.3 1.2 %copy-start.1 = (bf16[13,80,128]{2,1,0:T(8,128)(2,1)}, bf16[13,80,128]{2,1,0:T(8,128)(2,1)S(1)}, u32[]{:S(2)}) copy-start(bf16[13,80,128]{2,1,0:T(8,128)(2,1)S(1)} %collective-permute-done.prev_box) | copy-start | bytes 798724
  20.4 0.7 copy-start.2
  38.0 21.3 %collective-permute-start.3 = (bf16[2,13,80,128]{3,2,1,0:T(8,128)(2,1)S(1)}, bf16[2,13,80,128]{3,2,1,0:T(8,128)(2,1)S(1)}, u32[]{:S(2)}, u32[]{:S(2)}) collective-permute-start(bf16[2,13,80,128]{3,2,1,0:T(8,128)(2,1)S(1)} %slice.7), channel_id=1, source_target_pairs={{1,0},{2,1},{3,2},{4,3},{5,4},{6,5},{7,6},{8,7},{9,8},{10,9},{11,1... | collective-permute-start | bytes 1597448 | tf_op jit(solution)/shard_map/ppermute | solution.py:336
  46.9 12.3 %collective-permute-start.2 = (bf16[1,13,80,128]{3,2,1,0:T(8,128)(2,1)S(1)}, bf16[1,13,80,128]{3,2,1,0:T(8,128)(2,1)S(1)}, u32[]{:S(2)}, u32[]{:S(2)}) collective-permute-start(bf16[1,13,80,128]{3,2,1,0:T(8,128)(2,1)S(1)} %slice.6), channel_id=1, source_target_pairs={{0,1},{1,2},{2,3},{3,4},{4,5},{5,6},{6,7},{7,8},{8,9},{9,10},{10,1... | collective-permute-start | bytes 798728 | tf_op jit(solution)/shard_map/ppermute | solution.py:335
  59.3 0.7 copy-start.3
  59.3 0.9 %copy-start = (bf16[2,13,80,128]{3,2,1,0:T(8,128)(2,1)}, bf16[2,13,80,128]{3,2,1,0:T(8,128)(2,1)S(1)}, u32[]{:S(2)}) copy-start(bf16[2,13,80,128]{3,2,1,0:T(8,128)(2,1)S(1)} %collective-permute-done.3.next_results) | copy-start | bytes 1597444

commit v2 on v1

v2 whole, which is shorter than its diff:
```python
import functools

import jax
import jax.numpy as jnp
import ml_dtypes
import numpy as np
from jax import lax
from jax.experimental import pallas as pl
from jax.experimental.pallas import tpu as pltpu
from jax.sharding import PartitionSpec as P

AXES = ("gx", "gy", "gz")
DEVICES = 128
SPINS = 2
EDGE = 40
PLANE = EDGE * EDGE
CELLS = EDGE * PLANE
GRID = (768, 384, 384)
BOX_DEV = 4
CAP = 7
SCREEN = 0.001

LANE = 128
TILES = 13
WIDTH = TILES * LANE
OFF = (WIDTH - PLANE) // 2
MARGIN = 7 * LANE
WIDE = WIDTH + 2 * MARGIN
ROWS = SPINS * EDGE
PAIR_ROWS = BOX_DEV * 2 * ROWS
OUT_ROWS = SPINS * CELLS // LANE
BATCHES = ((0, 1), (1, 2), (3, 1))
GROUP = 25
EMPTY = MARGIN // LANE
SPREAD = WIDE // LANE
MESH = pl.DeviceIdType.MESH


def tables():
    counter = np.arange(EDGE, dtype=np.float64) + 1.0
    angles = np.pi * counter[:, None] * counter[None, :] / (EDGE + 1.0)
    sine = (np.sqrt(2.0 / (EDGE + 1.0)) * np.sin(angles)).astype(ml_dtypes.bfloat16)
    levels = 2.0 - 2.0 * np.cos(np.pi * counter / (EDGE + 1.0))
    plane = (levels[:, None] + levels[None, :]).reshape(-1)
    inverse = np.zeros((EDGE, WIDTH), np.float32)
    inverse[:, OFF : OFF + PLANE] = 1.0 / (levels[:, None] + plane[None, :] + SCREEN)
    inverse = np.concatenate([inverse, inverse], axis=0)
    sine32 = sine.astype(np.float32)
    first = np.kron(np.eye(4, dtype=np.float32), sine32).astype(ml_dtypes.bfloat16)
    both = np.zeros((WIDTH, WIDTH), np.float32)
    both[OFF : OFF + PLANE, OFF : OFF + PLANE] = np.kron(sine32, sine32)
    both = both.astype(ml_dtypes.bfloat16)
    cells = np.full((2, WIDTH), -1000, np.int32)
    cells[0, OFF : OFF + PLANE] = np.arange(PLANE) // EDGE
    cells[1, OFF : OFF + PLANE] = np.arange(PLANE) % EDGE
    return first, both, inverse, cells


def device_number():
    index = lax.axis_index(AXES[0])
    for name in AXES[1:]:
        index = index * lax.axis_size(name) + lax.axis_index(name)
    return index


def count(dest, first_box, device):
    total = 0
    for number in range(BOX_DEV):
        total = total + (dest[first_box + number] == device).astype(jnp.int32)
    return total


def position(backs, aheads, rank):
    place = backs + rank
    return place + jnp.where((place >= 2) & (aheads > 0), 1, 0)


def boxes_by_position(dest, device):
    base = device * BOX_DEV
    backs = count(dest, base, device - 1)
    aheads = count(dest, base, device + 1)
    order = [0] * BOX_DEV
    back_rank = stay_rank = 0
    for number in range(BOX_DEV):
        goal = dest[base + number]
        back = goal < device
        ahead = goal > device
        place = jnp.where(back, back_rank, jnp.where(ahead, 2, position(backs, aheads, stay_rank)))
        back_rank = back_rank + back.astype(jnp.int32)
        stay_rank = stay_rank + (goal == device).astype(jnp.int32)
        for spot in range(BOX_DEV):
            order[spot] = order[spot] + jnp.where(place == spot, number, 0)
    return order


def slot_sources(dest, device):
    base = device * BOX_DEV
    last = DEVICES - 1
    backs = count(dest, base, device - 1)
    aheads = count(dest, base, device + 1)
    stays = BOX_DEV - backs - aheads
    behind = jnp.maximum(device - 1, 0) * BOX_DEV
    front = jnp.minimum(device + 1, last) * BOX_DEV
    from_prev = jnp.where(device > 0, count(dest, behind, device), 0)
    from_next = jnp.where(device < last, count(dest, front, device), 0)
    sources = []
    for slot in range(CAP):
        rank = slot - from_prev
        late = rank - stays
        sources.append(
            jnp.where(
                rank < 0,
                4,
                jnp.where(
                    late < 0,
                    position(backs, aheads, rank),
                    jnp.where(late < from_next, 5 + late, 7),
                ),
            )
        )
    return sources


def shared_box(partners, device, other):
    inside = jnp.clip(other, 0, DEVICES - 1) * BOX_DEV
    chosen = 0
    for number in range(BOX_DEV):
        for which in range(2):
            partner = partners[which, inside + number] - device * BOX_DEV
            chosen = jnp.where((partner >= 0) & (partner < BOX_DEV), partner, chosen)
    return chosen


def wrapped(difference, extent):
    half = difference + extent // 2
    half = jnp.where(half < 0, half + extent, half)
    half = jnp.where(half >= extent, half - extent, half)
    return half - extent // 2


def pick(values, index):
    chosen = values[0]
    for number in range(1, len(values)):
        chosen = jnp.where(index == number, values[number], chosen)
    return chosen


def unpack_rows(orbitals, lines, boxes):
    def pair(number, carry):
        start = pl.multiple_of(number * 2 * PLANE, LANE)
        for spin in range(SPINS):
            cells = orbitals[spin, :, pl.ds(start, 2 * PLANE)].astype(jnp.float32)
            even = pltpu.roll(cells[:, :WIDTH], OFF, 1)
            odd = pltpu.roll(cells[:, 2 * PLANE - WIDTH :], WIDTH - OFF, 1)
            row = spin * EDGE + 2 * number
            for tile in range(TILES):
                span = slice(tile * LANE, (tile + 1) * LANE)
                lines[tile, pl.ds(row, BOX_DEV, stride=ROWS), :] = even[:, span]
                lines[tile, pl.ds(row + 1, BOX_DEV, stride=ROWS), :] = odd[:, span]
        return carry

    lax.fori_loop(0, EDGE // 2, pair, 0)
    for box in range(BOX_DEV):
        for tile in range(TILES):
            value = lines[tile, box * ROWS : (box + 1) * ROWS, :]
            boxes[box * SPREAD + EMPTY + tile] = value.astype(jnp.bfloat16)


def shift_pair(boxes, moved, density, cells, center, partner, delta, pair_row):
    flat = MARGIN - (delta[1] * EDGE + delta[2])
    column = flat // LANE
    turn = flat - column * LANE
    pair_row = pl.multiple_of(pair_row, ROWS)
    keep = lax.broadcasted_iota(jnp.int32, (ROWS, LANE), 1) < LANE - turn
    row = lax.broadcasted_iota(jnp.int32, (ROWS, ROWS), 0)
    source = lax.broadcasted_iota(jnp.int32, (ROWS, ROWS), 1)
    same = (row >= EDGE) == (source >= EDGE)
    shifter = (same & (source == row - delta[0])).astype(jnp.float32).astype(jnp.bfloat16)
    first_tile = partner * SPREAD + column
    wide = jnp.concatenate([boxes[first_tile + tile] for tile in range(TILES + 1)], axis=1)
    wide = jnp.dot(shifter, wide, preferred_element_type=jnp.float32)
    turned = [
        pltpu.roll(wide[:, tile * LANE : (tile + 1) * LANE], LANE - turn, 1)
        for tile in range(TILES + 1)
    ]
    for tile in range(TILES):
        span = slice(tile * LANE, (tile + 1) * LANE)
        second = cells[0:1, span] - delta[1]
        third = cells[1:2, span] - delta[2]
        inside = (second >= 0) & (second < EDGE) & (third >= 0) & (third < EDGE)
        inside = inside & (cells[0:1, span] >= 0)
        value = jnp.where(inside, jnp.where(keep, turned[tile], turned[tile + 1]), 0.0)
        product = boxes[center * SPREAD + EMPTY + tile].astype(jnp.float32) * value
        moved[pl.ds(pair_row, ROWS), span] = value
        density[pl.ds(pair_row, ROWS), span] = product.astype(jnp.bfloat16)


def by_chunk(body):
    def step(number, carry):
        body(pl.multiple_of(number * 256, 256), 256)
        return carry

    lax.fori_loop(0, WIDTH // 256, step, 0)
    body(WIDTH // 256 * 256, WIDTH % 256)


def solve(density, work, first, both, inverse, low, rows):
    span = slice(low, low + rows)
    for block in range(rows // (2 * ROWS)):
        part = slice(low + block * 2 * ROWS, low + (block + 1) * 2 * ROWS)
        work[part, :] = jnp.dot(
            first[...], density[part, :], preferred_element_type=jnp.float32
        ).astype(jnp.bfloat16)

    def forward(start, size):
        cut = pl.ds(start, size)
        out = jnp.dot(work[span, :], both[:, cut], preferred_element_type=jnp.float32)
        out = out.reshape(rows // ROWS, ROWS, size) * inverse[:, cut][None]
        density[span, cut] = out.reshape(rows, size).astype(jnp.bfloat16)

    def backward(start, size):
        cut = pl.ds(start, size)
        out = jnp.dot(density[span, :], both[:, cut], preferred_element_type=jnp.float32)
        work[span, cut] = out.astype(jnp.bfloat16)

    by_chunk(forward)
    by_chunk(backward)


def flatten_rows(lines, place):
    half = EDGE // 2
    lanes = lax.broadcasted_iota(jnp.int32, (half, LANE), 1)
    for spin in range(SPINS):
        even = [
            pltpu.roll(lines[tile, pl.ds(spin * EDGE, half, stride=2), :], LANE - OFF, 1)
            for tile in range(TILES)
        ]
        odd = [
            pltpu.roll(lines[tile, pl.ds(spin * EDGE + 1, half, stride=2), :], OFF, 1)
            for tile in range(TILES)
        ]
        for tile in range(TILES - 1):
            place(2 * tile + spin, jnp.where(lanes < LANE - OFF, even[tile], even[tile + 1]))
        place(2 * (TILES - 1) + spin, jnp.where(lanes < LANE // 2, even[TILES - 1], odd[0]))
        for tile in range(1, TILES):
            place(
                2 * (TILES - 1 + tile) + spin,
                jnp.where(lanes < OFF, odd[tile - 1], odd[tile]),
            )


def mesh_place(device):
    gz = lax.axis_size(AXES[2])
    gy = lax.axis_size(AXES[1])
    return (device // (gy * gz), (device // gz) % gy, device % gz)


def solve_kernel(
    dest, partners, anchors, orbitals, first, both_hbm, inverse, cells,
    results, arrived,
    boxes, moved, density, work, both, lines, box_out, box_in, sends,
    table_sem, box_send, box_recv, move_send, move_recv,
):
    device = device_number()
    following = mesh_place((device + 1) % DEVICES)
    previous = mesh_place((device + DEVICES - 1) % DEVICES)
    barrier = pltpu.get_barrier_semaphore()
    for other in (following, previous):
        pl.semaphore_signal(barrier, inc=1, device_id=other, device_id_type=MESH)
    table = pltpu.make_async_copy(both_hbm, both, table_sem)
    table.start()
    blank = jnp.zeros((ROWS, LANE), jnp.bfloat16)
    for box in range(BOX_DEV + 2):
        for tile in range(EMPTY):
            boxes[box * SPREAD + tile] = blank
            boxes[box * SPREAD + EMPTY + TILES + tile] = blank
    unpack_rows(orbitals, lines, boxes)
    box_copies = []
    for way, (other, target) in enumerate(((device + 1, following), (device - 1, previous))):
        chosen = shared_box(partners, device, other)
        for tile in range(TILES):
            box_out[way, tile] = boxes[chosen * SPREAD + EMPTY + tile]
        if way == 0:
            pl.semaphore_wait(barrier, 2)
        copy = pltpu.make_async_remote_copy(
            src_ref=box_out.at[way], dst_ref=box_in.at[way],
            send_sem=box_send.at[way], recv_sem=box_recv.at[way],
            device_id=target, device_id_type=MESH,
        )
        copy.start()
        box_copies.append(copy)
    order = boxes_by_position(dest, device)
    base = device * BOX_DEV
    for way, copy in enumerate(box_copies):
        copy.wait()
        for tile in range(TILES):
            boxes[(BOX_DEV + way) * SPREAD + EMPTY + tile] = box_in[way, tile]

    def pair(number, carry):
        spot = number // 2
        which = number % 2
        local_box = pick(order, spot)
        box = base + local_box
        partner = partners[which, box]
        local = partner - base
        place = jnp.where(local < 0, 4, jnp.where(local >= BOX_DEV, 5, local))
        delta = [wrapped(anchors[dim, partner] - anchors[dim, box], GRID[dim]) for dim in range(3)]
        shift_pair(
            boxes, moved, density, cells, local_box, place, delta, number * ROWS
        )
        return carry

    lax.fori_loop(0, 2 * BOX_DEV, pair, 0)
    table.wait()
    moves = []
    for begin, number in BATCHES:
        solve(density, work, first, both, inverse, begin * 2 * ROWS, number * 2 * ROWS)
        for spot in range(begin, begin + number):
            span = slice(spot * 2 * ROWS, (spot + 1) * 2 * ROWS)
            potential = jnp.dot(first[...], work[span, :], preferred_element_type=jnp.float32)
            terms = potential * moved[span, :]
            total = terms[:ROWS] + terms[ROWS:]
            for tile in range(TILES):
                lines[tile, :ROWS, :] = total[:, tile * LANE : (tile + 1) * LANE]

            def place(row, value):
                results[spot, pl.ds(row, EDGE // 2, stride=2 * (2 * TILES - 1)), :] = value

            flatten_rows(lines, place)
            if spot < 3:
                sends[spot] = results[spot].astype(jnp.bfloat16)
                copy = pltpu.make_async_remote_copy(
                    src_ref=sends.at[spot], dst_ref=arrived.at[spot],
                    send_sem=move_send.at[spot], recv_sem=move_recv.at[spot],
                    device_id=previous if spot < 2 else following, device_id_type=MESH,
                )
                copy.start()
                moves.append(copy)
    for copy in moves:
        copy.wait()


def assemble_kernel(dest, results, arrived, out, wide):
    device = device_number()
    slot = pl.program_id(0)
    source = pick(slot_sources(dest, device), slot)

    @pl.when(slot == 0)
    def _():
        wide[...] = arrived[...].astype(jnp.float32)

    def copy(source_ref):
        def group(number, carry):
            row = number * 2 * GROUP
            column = number * GROUP * LANE
            for tile in range(GROUP):
                start = pl.multiple_of(column + tile * LANE, LANE)
                out[0, :, pl.ds(start, LANE)] = source_ref[pl.ds(row + 2 * tile, SPINS), :]
            return carry

        lax.fori_loop(0, CELLS // (GROUP * LANE), group, 0)

    @pl.when(source < BOX_DEV)
    def _():
        copy(results.at[jnp.minimum(source, BOX_DEV - 1)])

    @pl.when((source >= BOX_DEV) & (source < 7))
    def _():
        copy(wide.at[jnp.where(source == 4, 2, jnp.clip(source - 5, 0, 1))])

    @pl.when(source == 7)
    def _():
        out[...] = jnp.zeros(out.shape, jnp.float32)


VMEM_LIMIT = 56 * 1024 * 1024


def shards(orbitals, dest, partners, anchors):
    first, both, inverse, cells = (jnp.asarray(table) for table in tables())
    partners = partners.T
    anchors = anchors.T
    smem = pl.BlockSpec(memory_space=pltpu.SMEM)
    vmem = pl.BlockSpec(memory_space=pltpu.VMEM)
    hbm = pl.BlockSpec(memory_space=pl.ANY)
    results, arrived = pl.pallas_call(
        solve_kernel,
        out_shape=(
            jax.ShapeDtypeStruct((BOX_DEV, OUT_ROWS, LANE), jnp.float32),
            jax.ShapeDtypeStruct((3, OUT_ROWS, LANE), jnp.bfloat16),
        ),
        in_specs=[smem] * 3 + [vmem, vmem, hbm, vmem, vmem],
        out_specs=[vmem] * 2,
        scratch_shapes=[
            pltpu.VMEM(((BOX_DEV + 2) * SPREAD, ROWS, LANE), jnp.bfloat16),
            pltpu.VMEM((PAIR_ROWS, WIDTH), jnp.float32),
            pltpu.VMEM((PAIR_ROWS, WIDTH), jnp.bfloat16),
            pltpu.VMEM((PAIR_ROWS, WIDTH), jnp.bfloat16),
            pltpu.VMEM((WIDTH, WIDTH), jnp.bfloat16),
            pltpu.VMEM((TILES, BOX_DEV * ROWS, LANE), jnp.float32),
            pltpu.VMEM((2, TILES, ROWS, LANE), jnp.bfloat16),
            pltpu.VMEM((2, TILES, ROWS, LANE), jnp.bfloat16),
            pltpu.VMEM((3, OUT_ROWS, LANE), jnp.bfloat16),
            pltpu.SemaphoreType.DMA,
            pltpu.SemaphoreType.DMA((2,)),
            pltpu.SemaphoreType.DMA((2,)),
            pltpu.SemaphoreType.DMA((3,)),
            pltpu.SemaphoreType.DMA((3,)),
        ],
        compiler_params=pltpu.CompilerParams(
            vmem_limit_bytes=VMEM_LIMIT, collective_id=0, has_side_effects=True
        ),
    )(dest, partners, anchors, orbitals, first, both, inverse, cells)
    out = pl.pallas_call(
        assemble_kernel,
        out_shape=jax.ShapeDtypeStruct((CAP, SPINS, CELLS), jnp.float32),
        grid=(CAP,),
        in_specs=[smem, vmem, vmem],
        out_specs=pl.BlockSpec((1, SPINS, CELLS), lambda slot: (slot, 0, 0)),
        scratch_shapes=[pltpu.VMEM((3, OUT_ROWS, LANE), jnp.float32)],
        compiler_params=pltpu.CompilerParams(vmem_limit_bytes=16 * 1024 * 1024),
    )(dest, results, arrived)
    return jnp.transpose(out, (1, 0, 2))


def solution(mesh):
    return jax.shard_map(
        shards,
        mesh=mesh,
        in_specs=(P(None, AXES, None), P(), P(), P()),
        out_specs=P(None, AXES, None),
        check_vma=False,
    )
```

time: 77.9 us -> 53.3 us (0.68)
  the two profiles are of different devices: /device:TPU:96 before, /device:TPU:0 now
where the time goes in v2:
time: 53.3 us; the launch traced here: 53.1 us
  Pallas kernels  50.3 us (94%)
  local copies, waits for them, and re-layouts  2.7 us (5%)
    pallas_call x1, Pallas kernels, shards(): pl.pallas_call(solve_kernel, out_shape=(jax.ShapeDtypeStruct((BOX_DEV, OU...  44.2 us
    pallas_call x1, Pallas kernels, shards(): pl.pallas_call(assemble_kernel, out_shape=jax.ShapeDtypeStruct((CAP, SPIN...  6.1 us
    unnamed x6, local copies, waits for them, and re-layouts  2.7 us

profile of v2, /device:TPU:0, one launch (start us, length us, event | category | flops | bytes accessed | tf_op | source)
XLA Modules:
  0.0 53.1 jit_solution(3648185925294609266)
XLA Ops:
  0.0 0.0 copy-start.2
  0.0 44.2 %shard_map.82 = (f32[4,1000,128]{2,1,0:T(8,128)}, bf16[3,1000,128]{2,1,0:T(8,128)(2,1)}) custom-call(s32[512]{0:T(512)} %dest.3, s32[2,512]{1,0:T(2,128)} %bitcast.4, s32[3,512]{1,0:T(4,128)} %bitcast.3, bf16[2,4,64000]{2,1,0:T(4,128)(2,1)} %orbitals.1, bf16[160,160]{1,0:T(8,128)(2,1)} %constant.8.clone.first, bf16[1664,1664]{1,0:T(8,128)(2,1)} %constant.9.clone.both_hbm, ...), custom_call_target="tpu_custom_call" | custom-call | tf_op jit(solution)/shard_map/pallas_call | solution.py:386
  44.2 0.0 copy-done.2
  44.3 0.0 copy-start
  44.3 1.6 %copy-done = f32[4,1000,128]{2,1,0:T(8,128)S(1)} copy-done((f32[4,1000,128]{2,1,0:T(8,128)S(1)}, f32[4,1000,128]{2,1,0:T(8,128)}, u32[]{:S(2)}) %copy-start) | copy-done | bytes 2048024
  45.8 0.0 copy-start.1
  45.8 1.1 %copy-done.1 = bf16[3,1000,128]{2,1,0:T(8,128)(2,1)S(1)} copy-done((bf16[3,1000,128]{2,1,0:T(8,128)(2,1)S(1)}, bf16[3,1000,128]{2,1,0:T(8,128)(2,1)}, u32[]{:S(2)}) %copy-start.1) | copy-done | bytes 768024
  47.0 6.1 %shard_map.83 = f32[7,2,64000]{2,1,0:T(2,128)} custom-call(s32[512]{0:T(512)S(1)} %copy-done.2, f32[4,1000,128]{2,1,0:T(8,128)S(1)} %copy-done, bf16[3,1000,128]{2,1,0:T(8,128)(2,1)S(1)} %copy-done.1), custom_call_target="tpu_custom_call" | custom-call | tf_op jit(solution)/shard_map/pallas_call | solution.py:414
Async XLA Ops:
  0.0 44.2 %copy-start.2 = (s32[512]{0:T(512)S(1)}, s32[512]{0:T(512)}, u32[]{:S(2)}) copy-start(s32[512]{0:T(512)} %dest.3) | copy-start | bytes 6148
  44.3 1.6 %copy-start = (f32[4,1000,128]{2,1,0:T(8,128)S(1)}, f32[4,1000,128]{2,1,0:T(8,128)}, u32[]{:S(2)}) copy-start(f32[4,1000,128]{2,1,0:T(8,128)} %get-tuple-element.7.results) | copy-start | bytes 6144004
  45.8 1.1 %copy-start.1 = (bf16[3,1000,128]{2,1,0:T(8,128)(2,1)S(1)}, bf16[3,1000,128]{2,1,0:T(8,128)(2,1)}, u32[]{:S(2)}) copy-start(bf16[3,1000,128]{2,1,0:T(8,128)(2,1)} %get-tuple-element.8.arrived) | copy-start | bytes 2304004

commit v3 on v2

--- a/solution.py
+++ b/solution.py
@@ -29,7 +29,6 @@
 ROWS = SPINS * EDGE
 PAIR_ROWS = BOX_DEV * 2 * ROWS
 OUT_ROWS = SPINS * CELLS // LANE
-BATCHES = ((0, 1), (1, 2), (3, 1))
 GROUP = 25
 EMPTY = MARGIN // LANE
 SPREAD = WIDE // LANE
@@ -110,11 +109,11 @@
         sources.append(
             jnp.where(
                 rank < 0,
-                4,
+                6,
                 jnp.where(
                     late < 0,
                     position(backs, aheads, rank),
-                    jnp.where(late < from_next, 5 + late, 7),
+                    jnp.where(late < from_next, 4 + late, 7),
                 ),
             )
         )
@@ -196,12 +195,8 @@
 
 
 def by_chunk(body):
-    def step(number, carry):
-        body(pl.multiple_of(number * 256, 256), 256)
-        return carry
-
-    lax.fori_loop(0, WIDTH // 256, step, 0)
-    body(WIDTH // 256 * 256, WIDTH % 256)
+    for start in range(0, WIDTH, 256):
+        body(start, min(256, WIDTH - start))
 
 
 def solve(density, work, first, both, inverse, low, rows):
@@ -249,6 +244,18 @@
             )
 
 
+def tile_spins(flat, ready):
+    def group(number, carry):
+        row = number * 2 * GROUP
+        column = number * GROUP * LANE
+        for tile in range(GROUP):
+            start = pl.multiple_of(column + tile * LANE, LANE)
+            ready[:, pl.ds(start, LANE)] = flat[pl.ds(row + 2 * tile, SPINS), :]
+        return carry
+
+    lax.fori_loop(0, CELLS // (GROUP * LANE), group, 0)
+
+
 def mesh_place(device):
     gz = lax.axis_size(AXES[2])
     gy = lax.axis_size(AXES[1])
@@ -257,44 +264,77 @@
 
 def solve_kernel(
     dest, partners, anchors, orbitals, first, both_hbm, inverse, cells,
-    results, arrived,
-    boxes, moved, density, work, both, lines, box_out, box_in, sends,
+    ready,
+    boxes, moved, density, work, both, lines, flat, box_out, box_in, sends, arrived,
     table_sem, box_send, box_recv, move_send, move_recv,
 ):
     device = device_number()
-    following = mesh_place((device + 1) % DEVICES)
-    previous = mesh_place((device + DEVICES - 1) % DEVICES)
+    has_next = device < DEVICES - 1
+    has_prev = device > 0
+    following = mesh_place(jnp.minimum(device + 1, DEVICES - 1))
+    previous = mesh_place(jnp.maximum(device - 1, 0))
     barrier = pltpu.get_barrier_semaphore()
-    for other in (following, previous):
-        pl.semaphore_signal(barrier, inc=1, device_id=other, device_id_type=MESH)
+
+    @pl.when(has_next)
+    def _():
+        pl.semaphore_signal(barrier, inc=1, device_id=following, device_id_type=MESH)
+
+    @pl.when(has_prev)
+    def _():
+        pl.semaphore_signal(barrier, inc=1, device_id=previous, device_id_type=MESH)
+
     table = pltpu.make_async_copy(both_hbm, both, table_sem)
     table.start()
+
+    def box_copy(way):
+        return pltpu.make_async_remote_copy(
+            src_ref=box_out.at[way], dst_ref=box_in.at[way],
+            send_sem=box_send.at[way], recv_sem=box_recv.at[way],
+            device_id=(following, previous)[way], device_id_type=MESH,
+        )
+
+    def move_copy(spot):
+        return pltpu.make_async_remote_copy(
+            src_ref=sends.at[spot], dst_ref=arrived.at[spot],
+            send_sem=move_send.at[spot], recv_sem=move_recv.at[spot],
+            device_id=previous if spot < 2 else following, device_id_type=MESH,
+        )
+
     blank = jnp.zeros((ROWS, LANE), jnp.bfloat16)
     for box in range(BOX_DEV + 2):
         for tile in range(EMPTY):
             boxes[box * SPREAD + tile] = blank
             boxes[box * SPREAD + EMPTY + TILES + tile] = blank
     unpack_rows(orbitals, lines, boxes)
-    box_copies = []
-    for way, (other, target) in enumerate(((device + 1, following), (device - 1, previous))):
+    for way, other in enumerate((device + 1, device - 1)):
         chosen = shared_box(partners, device, other)
         for tile in range(TILES):
             box_out[way, tile] = boxes[chosen * SPREAD + EMPTY + tile]
-        if way == 0:
-            pl.semaphore_wait(barrier, 2)
-        copy = pltpu.make_async_remote_copy(
-            src_ref=box_out.at[way], dst_ref=box_in.at[way],
-            send_sem=box_send.at[way], recv_sem=box_recv.at[way],
-            device_id=target, device_id_type=MESH,
-        )
-        copy.start()
-        box_copies.append(copy)
+
+    pl.semaphore_wait(barrier, has_next.astype(jnp.int32) + has_prev.astype(jnp.int32))
+
+    @pl.when(has_next)
+    def _():
+        box_copy(0).start()
+
+    @pl.when(has_prev)
+    def _():
+        box_copy(1).start()
+
     order = boxes_by_position(dest, device)
     base = device * BOX_DEV
-    for way, copy in enumerate(box_copies):
-        copy.wait()
+
+    @pl.when(has_prev)
+    def _():
+        box_copy(0).wait_recv()
         for tile in range(TILES):
-            boxes[(BOX_DEV + way) * SPREAD + EMPTY + tile] = box_in[way, tile]
+            boxes[BOX_DEV * SPREAD + EMPTY + tile] = box_in[0, tile]
+
+    @pl.when(has_next)
+    def _():
+        box_copy(1).wait_recv()
+        for tile in range(TILES):
+            boxes[(BOX_DEV + 1) * SPREAD + EMPTY + tile] = box_in[1, tile]
 
     def pair(number, carry):
         spot = number // 2
@@ -305,92 +345,88 @@
         local = partner - base
         place = jnp.where(local < 0, 4, jnp.where(local >= BOX_DEV, 5, local))
         delta = [wrapped(anchors[dim, partner] - anchors[dim, box], GRID[dim]) for dim in range(3)]
-        shift_pair(
-            boxes, moved, density, cells, local_box, place, delta, number * ROWS
-        )
+        shift_pair(boxes, moved, density, cells, local_box, place, delta, number * ROWS)
         return carry
 
     lax.fori_loop(0, 2 * BOX_DEV, pair, 0)
     table.wait()
-    moves = []
-    for begin, number in BATCHES:
-        solve(density, work, first, both, inverse, begin * 2 * ROWS, number * 2 * ROWS)
-        for spot in range(begin, begin + number):
-            span = slice(spot * 2 * ROWS, (spot + 1) * 2 * ROWS)
-            potential = jnp.dot(first[...], work[span, :], preferred_element_type=jnp.float32)
-            terms = potential * moved[span, :]
-            total = terms[:ROWS] + terms[ROWS:]
-            for tile in range(TILES):
-                lines[tile, :ROWS, :] = total[:, tile * LANE : (tile + 1) * LANE]
-
-            def place(row, value):
-                results[spot, pl.ds(row, EDGE // 2, stride=2 * (2 * TILES - 1)), :] = value
-
-            flatten_rows(lines, place)
-            if spot < 3:
-                sends[spot] = results[spot].astype(jnp.bfloat16)
-                copy = pltpu.make_async_remote_copy(
-                    src_ref=sends.at[spot], dst_ref=arrived.at[spot],
-                    send_sem=move_send.at[spot], recv_sem=move_recv.at[spot],
-                    device_id=previous if spot < 2 else following, device_id_type=MESH,
-                )
-                copy.start()
-                moves.append(copy)
-    for copy in moves:
-        copy.wait()
-
-
-def assemble_kernel(dest, results, arrived, out, wide):
+    for spot in range(BOX_DEV):
+        solve(density, work, first, both, inverse, spot * 2 * ROWS, 2 * ROWS)
+        span = slice(spot * 2 * ROWS, (spot + 1) * 2 * ROWS)
+        potential = jnp.dot(first[...], work[span, :], preferred_element_type=jnp.float32)
+        terms = potential * moved[span, :]
+        total = terms[:ROWS] + terms[ROWS:]
+        for tile in range(TILES):
+            lines[tile, :ROWS, :] = total[:, tile * LANE : (tile + 1) * LANE]
+
+        def place(row, value):
+            flat[spot, pl.ds(row, EDGE // 2, stride=2 * (2 * TILES - 1)), :] = value
+
+        flatten_rows(lines, place)
+        if spot < 3:
+            sends[spot] = flat[spot].astype(jnp.bfloat16)
+
+            @pl.when(has_prev if spot < 2 else has_next)
+            def _():
+                move_copy(spot).start()
+
+    for spot in range(BOX_DEV):
+        tile_spins(flat.at[spot], ready.at[spot])
+    for spot in (0, 2, 1):
+        comes = has_next if spot < 2 else has_prev
+
+        @pl.when(comes)
+        def _():
+            move_copy(spot).wait_recv()
+            flat[spot] = arrived[spot].astype(jnp.float32)
+            tile_spins(flat.at[spot], ready.at[BOX_DEV + spot])
+
+    @pl.when(has_next)
+    def _():
+        box_copy(0).wait_send()
+        move_copy(2).wait_send()
+
+    @pl.when(has_prev)
+    def _():
+        box_copy(1).wait_send()
+        move_copy(0).wait_send()
+        move_copy(1).wait_send()
+
+
+def assemble_kernel(dest, ready, out, blank, sems):
     device = device_number()
-    slot = pl.program_id(0)
-    source = pick(slot_sources(dest, device), slot)
-
-    @pl.when(slot == 0)
-    def _():
-        wide[...] = arrived[...].astype(jnp.float32)
-
-    def copy(source_ref):
-        def group(number, carry):
-            row = number * 2 * GROUP
-            column = number * GROUP * LANE
-            for tile in range(GROUP):
-                start = pl.multiple_of(column + tile * LANE, LANE)
-                out[0, :, pl.ds(start, LANE)] = source_ref[pl.ds(row + 2 * tile, SPINS), :]
-            return carry
-
-        lax.fori_loop(0, CELLS // (GROUP * LANE), group, 0)
-
-    @pl.when(source < BOX_DEV)
-    def _():
-        copy(results.at[jnp.minimum(source, BOX_DEV - 1)])
-
-    @pl.when((source >= BOX_DEV) & (source < 7))
-    def _():
-        copy(wide.at[jnp.where(source == 4, 2, jnp.clip(source - 5, 0, 1))])
-
-    @pl.when(source == 7)
-    def _():
-        out[...] = jnp.zeros(out.shape, jnp.float32)
-
-
-VMEM_LIMIT = 56 * 1024 * 1024
+    blank[...] = jnp.zeros(blank.shape, jnp.float32)
+    for slot, source in enumerate(slot_sources(dest, device)):
+
+        @pl.when(source < CAP)
+        def _():
+            where = jnp.minimum(source, CAP - 1)
+            pltpu.make_async_copy(ready.at[where], out.at[slot], sems.at[slot]).start()
+
+        @pl.when(source == CAP)
+        def _():
+            pltpu.make_async_copy(blank, out.at[slot], sems.at[slot]).start()
+
+    for slot in range(CAP):
+        pltpu.make_async_copy(blank, out.at[slot], sems.at[slot]).wait()
+
+
+VMEM_LIMIT = 36 * 1024 * 1024
 
 
 def shards(orbitals, dest, partners, anchors):
     first, both, inverse, cells = (jnp.asarray(table) for table in tables())
+    both = pltpu.with_memory_space_constraint(both, pltpu.HBM)
     partners = partners.T
     anchors = anchors.T
     smem = pl.BlockSpec(memory_space=pltpu.SMEM)
     vmem = pl.BlockSpec(memory_space=pltpu.VMEM)
     hbm = pl.BlockSpec(memory_space=pl.ANY)
-    results, arrived = pl.pallas_call(
+    ready = pl.pallas_call(
         solve_kernel,
-        out_shape=(
-            jax.ShapeDtypeStruct((BOX_DEV, OUT_ROWS, LANE), jnp.float32),
-            jax.ShapeDtypeStruct((3, OUT_ROWS, LANE), jnp.bfloat16),
-        ),
-        in_specs=[smem] * 3 + [vmem, vmem, hbm, vmem, vmem],
-        out_specs=[vmem] * 2,
+        out_shape=jax.ShapeDtypeStruct((CAP, SPINS, CELLS), jnp.float32),
+        in_specs=[smem] * 3 + [vmem, vmem, pl.BlockSpec(memory_space=pltpu.HBM), vmem, vmem],
+        out_specs=vmem,
         scratch_shapes=[
             pltpu.VMEM(((BOX_DEV + 2) * SPREAD, ROWS, LANE), jnp.bfloat16),
             pltpu.VMEM((PAIR_ROWS, WIDTH), jnp.float32),
@@ -398,8 +434,10 @@
             pltpu.VMEM((PAIR_ROWS, WIDTH), jnp.bfloat16),
             pltpu.VMEM((WIDTH, WIDTH), jnp.bfloat16),
             pltpu.VMEM((TILES, BOX_DEV * ROWS, LANE), jnp.float32),
+            pltpu.VMEM((BOX_DEV, OUT_ROWS, LANE), jnp.float32),
             pltpu.VMEM((2, TILES, ROWS, LANE), jnp.bfloat16),
             pltpu.VMEM((2, TILES, ROWS, LANE), jnp.bfloat16),
+            pltpu.VMEM((3, OUT_ROWS, LANE), jnp.bfloat16),
             pltpu.VMEM((3, OUT_ROWS, LANE), jnp.bfloat16),
             pltpu.SemaphoreType.DMA,
             pltpu.SemaphoreType.DMA((2,)),
@@ -414,12 +452,14 @@
     out = pl.pallas_call(
         assemble_kernel,
         out_shape=jax.ShapeDtypeStruct((CAP, SPINS, CELLS), jnp.float32),
-        grid=(CAP,),
-        in_specs=[smem, vmem, vmem],
-        out_specs=pl.BlockSpec((1, SPINS, CELLS), lambda slot: (slot, 0, 0)),
-        scratch_shapes=[pltpu.VMEM((3, OUT_ROWS, LANE), jnp.float32)],
-        compiler_params=pltpu.CompilerParams(vmem_limit_bytes=16 * 1024 * 1024),
-    )(dest, results, arrived)
+        in_specs=[smem, hbm],
+        out_specs=hbm,
+        scratch_shapes=[
+            pltpu.VMEM((SPINS, CELLS), jnp.float32),
+            pltpu.SemaphoreType.DMA((CAP,)),
+        ],
+        compiler_params=pltpu.CompilerParams(vmem_limit_bytes=2 * 1024 * 1024),
+    )(dest, ready)
     return jnp.transpose(out, (1, 0, 2))
 
 

time: 53.3 us -> 45.9 us (0.86)
  the two profiles are of different devices: /device:TPU:0 before, /device:TPU:96 now
where the time goes in v3:
time: 45.9 us; the launch traced here: 45.5 us
  Pallas kernels  39.6 us (86%)
  local copies, waits for them, and re-layouts  5.92 us (13%)
    pallas_call x1, Pallas kernels, shards(): pl.pallas_call(solve_kernel, out_shape=jax.ShapeDtypeStruct((CAP, SPINS,...  37.1 us
    unnamed x14, local copies, waits for them, and re-layouts  5.92 us
    pallas_call x1, Pallas kernels, shards(): pl.pallas_call(assemble_kernel, out_shape=jax.ShapeDtypeStruct((CAP, SPIN...  2.47 us

profile of v3, /device:TPU:96, one launch (start us, length us, event | category | flops | bytes accessed | tf_op | source)
XLA Modules:
  0.0 45.5 jit_solution(12080641918667450465)
XLA Ops:
  0.0 0.0 copy-start
  0.0 1.2 %copy-done = bf16[2,4,64000]{2,1,0:T(4,128)(2,1)S(1)} copy-done((bf16[2,4,64000]{2,1,0:T(4,128)(2,1)S(1)}, bf16[2,4,64000]{2,1,0:T(4,128)(2,1)}, u32[]{:S(2)}) %copy-start) | copy-done | bytes 1024024
  1.2 0.0 copy-start.1
  1.2 1.0 %copy-done.1 = f32[80,1664]{1,0:T(8,128)S(1)} copy-done((f32[80,1664]{1,0:T(8,128)S(1)}, f32[80,1664]{1,0:T(8,128)}, u32[]{:S(2)}) %copy-start.1) | copy-done | bytes 532504
  2.3 0.0 copy-start.2
  2.3 0.9 %copy-done.2 = bf16[160,160]{1,0:T(8,128)(2,1)S(1)} copy-done((bf16[160,160]{1,0:T(8,128)(2,1)S(1)}, bf16[160,160]{1,0:T(8,128)(2,1)}, u32[]{:S(2)}) %copy-start.2) | copy-done | bytes 51224
  3.1 0.0 copy-start.3
  3.2 0.7 %copy-done.3 = s32[2,1664]{1,0:T(2,128)S(1)} copy-done((s32[2,1664]{1,0:T(2,128)S(1)}, s32[2,1664]{1,0:T(2,128)}, u32[]{:S(2)}) %copy-start.3) | copy-done | bytes 13336
  3.9 0.0 copy-start.4
  3.9 0.7 %copy-done.4 = s32[512]{0:T(512)S(1)} copy-done((s32[512]{0:T(512)S(1)}, s32[512]{0:T(512)}, u32[]{:S(2)}) %copy-start.4) | copy-done | bytes 2072
  4.5 0.0 copy-start.5
  4.5 0.7 %copy-done.5 = s32[512,3]{0,1:T(4,128)S(1)} copy-done((s32[512,3]{0,1:T(4,128)S(1)}, s32[512,3]{0,1:T(4,128)}, u32[]{:S(2)}) %copy-start.5) | copy-done | bytes 6168
  5.2 0.0 copy-start.6
  5.2 0.7 %copy-done.6 = s32[512,2]{0,1:T(2,128)S(1)} copy-done((s32[512,2]{0,1:T(2,128)S(1)}, s32[512,2]{0,1:T(2,128)}, u32[]{:S(2)}) %copy-start.6) | copy-done | bytes 4120
  5.9 37.1 %shard_map.82.ready = f32[7,2,64000]{2,1,0:T(2,128)S(1)} custom-call(s32[512]{0:T(512)S(1)} %copy-done.4, s32[2,512]{1,0:T(2,128)S(1)} %bitcast.4, s32[3,512]{1,0:T(4,128)S(1)} %bitcast.3, bf16[2,4,64000]{2,1,0:T(4,128)(2,1)S(1)} %copy-done, bf16[160,160]{1,0:T(8,128)(2,1)S(1)} %copy-done.2, bf16[1664,1664]{1,0:T(8,128)(2,1)} %constant.9.clone.both_hbm, ...), custom_call_target="tpu_custom_call" | custom-call | tf_op jit(solution)/shard_map/pallas_call | solution.py:425
  43.1 2.5 %shard_map.83 = f32[7,2,64000]{2,1,0:T(2,128)} custom-call(s32[512]{0:T(512)S(1)} %copy-done.4, f32[7,2,64000]{2,1,0:T(2,128)S(1)} %shard_map.82.ready), custom_call_target="tpu_custom_call" | custom-call | tf_op jit(solution)/shard_map/pallas_call | solution.py:452
Async XLA Ops:
  0.0 1.2 %copy-start = (bf16[2,4,64000]{2,1,0:T(4,128)(2,1)S(1)}, bf16[2,4,64000]{2,1,0:T(4,128)(2,1)}, u32[]{:S(2)}) copy-start(bf16[2,4,64000]{2,1,0:T(4,128)(2,1)} %orbitals.1) | copy-start | bytes 3072004
  1.2 1.0 %copy-start.1 = (f32[80,1664]{1,0:T(8,128)S(1)}, f32[80,1664]{1,0:T(8,128)}, u32[]{:S(2)}) copy-start(f32[80,1664]{1,0:T(8,128)} %constant.10.clone.inverse) | copy-start | bytes 1597444
  2.3 0.9 %copy-start.2 = (bf16[160,160]{1,0:T(8,128)(2,1)S(1)}, bf16[160,160]{1,0:T(8,128)(2,1)}, u32[]{:S(2)}) copy-start(bf16[160,160]{1,0:T(8,128)(2,1)} %constant.8.clone.first) | copy-start | bytes 153604
  3.1 0.7 %copy-start.3 = (s32[2,1664]{1,0:T(2,128)S(1)}, s32[2,1664]{1,0:T(2,128)}, u32[]{:S(2)}) copy-start(s32[2,1664]{1,0:T(2,128)} %constant.11.clone.cells) | copy-start | bytes 39940
  3.9 0.7 %copy-start.4 = (s32[512]{0:T(512)S(1)}, s32[512]{0:T(512)}, u32[]{:S(2)}) copy-start(s32[512]{0:T(512)} %dest.3) | copy-start | bytes 6148
  4.5 0.7 %copy-start.5 = (s32[512,3]{0,1:T(4,128)S(1)}, s32[512,3]{0,1:T(4,128)}, u32[]{:S(2)}) copy-start(s32[512,3]{0,1:T(4,128)} %param.11) | copy-start | bytes 18436
  5.2 0.7 %copy-start.6 = (s32[512,2]{0,1:T(2,128)S(1)}, s32[512,2]{0,1:T(2,128)}, u32[]{:S(2)}) copy-start(s32[512,2]{0,1:T(2,128)} %param.10) | copy-start | bytes 12292

commit v4 on v3

--- a/solution.py
+++ b/solution.py
@@ -11,6 +11,7 @@
 
 AXES = ("gx", "gy", "gz")
 DEVICES = 128
+BOXES = 512
 SPINS = 2
 EDGE = 40
 PLANE = EDGE * EDGE
@@ -158,7 +159,7 @@
                 lines[tile, pl.ds(row + 1, BOX_DEV, stride=ROWS), :] = odd[:, span]
         return carry
 
-    lax.fori_loop(0, EDGE // 2, pair, 0)
+    lax.fori_loop(0, EDGE // 2, pair, 0, unroll=4)
     for box in range(BOX_DEV):
         for tile in range(TILES):
             value = lines[tile, box * ROWS : (box + 1) * ROWS, :]
@@ -169,7 +170,6 @@
     flat = MARGIN - (delta[1] * EDGE + delta[2])
     column = flat // LANE
     turn = flat - column * LANE
-    pair_row = pl.multiple_of(pair_row, ROWS)
     keep = lax.broadcasted_iota(jnp.int32, (ROWS, LANE), 1) < LANE - turn
     row = lax.broadcasted_iota(jnp.int32, (ROWS, ROWS), 0)
     source = lax.broadcasted_iota(jnp.int32, (ROWS, ROWS), 1)
@@ -190,8 +190,8 @@
         inside = inside & (cells[0:1, span] >= 0)
         value = jnp.where(inside, jnp.where(keep, turned[tile], turned[tile + 1]), 0.0)
         product = boxes[center * SPREAD + EMPTY + tile].astype(jnp.float32) * value
-        moved[pl.ds(pair_row, ROWS), span] = value
-        density[pl.ds(pair_row, ROWS), span] = product.astype(jnp.bfloat16)
+        moved[pair_row : pair_row + ROWS, span] = value
+        density[pair_row : pair_row + ROWS, span] = product.astype(jnp.bfloat16)
 
 
 def by_chunk(body):
@@ -263,10 +263,11 @@
 
 
 def solve_kernel(
-    dest, partners, anchors, orbitals, first, both_hbm, inverse, cells,
+    dest_hbm, partners_hbm, anchors_hbm, orbitals_hbm, first_hbm, both_hbm, inverse_hbm, cells_hbm,
     ready,
+    dest, partners, anchors, orbitals, first, inverse, cells,
     boxes, moved, density, work, both, lines, flat, box_out, box_in, sends, arrived,
-    table_sem, box_send, box_recv, move_send, move_recv,
+    load_sems, box_send, box_recv, move_send, move_recv,
 ):
     device = device_number()
     has_next = device < DEVICES - 1
@@ -283,8 +284,23 @@
     def _():
         pl.semaphore_signal(barrier, inc=1, device_id=previous, device_id_type=MESH)
 
-    table = pltpu.make_async_copy(both_hbm, both, table_sem)
-    table.start()
+    loads = [
+        pltpu.make_async_copy(source, target, load_sems.at[number])
+        for number, (source, target) in enumerate(
+            (
+                (orbitals_hbm, orbitals),
+                (dest_hbm, dest),
+                (partners_hbm, partners),
+                (anchors_hbm, anchors),
+                (first_hbm, first),
+                (cells_hbm, cells),
+                (inverse_hbm, inverse),
+                (both_hbm, both),
+            )
+        )
+    ]
+    for load in loads:
+        load.start()
 
     def box_copy(way):
         return pltpu.make_async_remote_copy(
@@ -305,7 +321,10 @@
         for tile in range(EMPTY):
             boxes[box * SPREAD + tile] = blank
             boxes[box * SPREAD + EMPTY + TILES + tile] = blank
+    loads[0].wait()
     unpack_rows(orbitals, lines, boxes)
+    for load in loads[1:4]:
+        load.wait()
     for way, other in enumerate((device + 1, device - 1)):
         chosen = shared_box(partners, device, other)
         for tile in range(TILES):
@@ -336,21 +355,24 @@
         for tile in range(TILES):
             boxes[(BOX_DEV + 1) * SPREAD + EMPTY + tile] = box_in[1, tile]
 
-    def pair(number, carry):
-        spot = number // 2
-        which = number % 2
-        local_box = pick(order, spot)
-        box = base + local_box
-        partner = partners[which, box]
-        local = partner - base
-        place = jnp.where(local < 0, 4, jnp.where(local >= BOX_DEV, 5, local))
-        delta = [wrapped(anchors[dim, partner] - anchors[dim, box], GRID[dim]) for dim in range(3)]
-        shift_pair(boxes, moved, density, cells, local_box, place, delta, number * ROWS)
-        return carry
-
-    lax.fori_loop(0, 2 * BOX_DEV, pair, 0)
-    table.wait()
+    def shift_box(spot):
+        box = base + order[spot]
+        for which in range(2):
+            partner = partners[which, box]
+            local = partner - base
+            place = jnp.where(local < 0, 4, jnp.where(local >= BOX_DEV, 5, local))
+            delta = [
+                wrapped(anchors[dim, partner] - anchors[dim, box], GRID[dim]) for dim in range(3)
+            ]
+            row = (spot * 2 + which) * ROWS
+            shift_pair(boxes, moved, density, cells, order[spot], place, delta, row)
+
+    for load in loads[4:]:
+        load.wait()
+    shift_box(0)
     for spot in range(BOX_DEV):
+        if spot + 1 < BOX_DEV:
+            shift_box(spot + 1)
         solve(density, work, first, both, inverse, spot * 2 * ROWS, 2 * ROWS)
         span = slice(spot * 2 * ROWS, (spot + 1) * 2 * ROWS)
         potential = jnp.dot(first[...], work[span, :], preferred_element_type=jnp.float32)
@@ -416,18 +438,24 @@
 
 def shards(orbitals, dest, partners, anchors):
     first, both, inverse, cells = (jnp.asarray(table) for table in tables())
-    both = pltpu.with_memory_space_constraint(both, pltpu.HBM)
-    partners = partners.T
-    anchors = anchors.T
+    operands = (dest, partners.T, anchors.T, orbitals, first, both, inverse, cells)
+    operands = [pltpu.with_memory_space_constraint(operand, pltpu.HBM) for operand in operands]
     smem = pl.BlockSpec(memory_space=pltpu.SMEM)
     vmem = pl.BlockSpec(memory_space=pltpu.VMEM)
     hbm = pl.BlockSpec(memory_space=pl.ANY)
     ready = pl.pallas_call(
         solve_kernel,
         out_shape=jax.ShapeDtypeStruct((CAP, SPINS, CELLS), jnp.float32),
-        in_specs=[smem] * 3 + [vmem, vmem, pl.BlockSpec(memory_space=pltpu.HBM), vmem, vmem],
+        in_specs=[pl.BlockSpec(memory_space=pltpu.HBM)] * 8,
         out_specs=vmem,
         scratch_shapes=[
+            pltpu.SMEM((BOXES,), jnp.int32),
+            pltpu.SMEM((2, BOXES), jnp.int32),
+            pltpu.SMEM((3, BOXES), jnp.int32),
+            pltpu.VMEM((SPINS, BOX_DEV, CELLS), jnp.bfloat16),
+            pltpu.VMEM(first.shape, first.dtype),
+            pltpu.VMEM(inverse.shape, inverse.dtype),
+            pltpu.VMEM(cells.shape, cells.dtype),
             pltpu.VMEM(((BOX_DEV + 2) * SPREAD, ROWS, LANE), jnp.bfloat16),
             pltpu.VMEM((PAIR_ROWS, WIDTH), jnp.float32),
             pltpu.VMEM((PAIR_ROWS, WIDTH), jnp.bfloat16),
@@ -439,7 +467,7 @@
             pltpu.VMEM((2, TILES, ROWS, LANE), jnp.bfloat16),
             pltpu.VMEM((3, OUT_ROWS, LANE), jnp.bfloat16),
             pltpu.VMEM((3, OUT_ROWS, LANE), jnp.bfloat16),
-            pltpu.SemaphoreType.DMA,
+            pltpu.SemaphoreType.DMA((8,)),
             pltpu.SemaphoreType.DMA((2,)),
             pltpu.SemaphoreType.DMA((2,)),
             pltpu.SemaphoreType.DMA((3,)),
@@ -448,7 +476,7 @@
         compiler_params=pltpu.CompilerParams(
             vmem_limit_bytes=VMEM_LIMIT, collective_id=0, has_side_effects=True
         ),
-    )(dest, partners, anchors, orbitals, first, both, inverse, cells)
+    )(*operands)
     out = pl.pallas_call(
         assemble_kernel,
         out_shape=jax.ShapeDtypeStruct((CAP, SPINS, CELLS), jnp.float32),

time: 45.9 us -> 36.7 us (0.80)
  local copies, waits for them, and re-layouts: 5.92 us -> 0.01 us
  Pallas kernels: 39.6 us -> 36.6 us
    unnamed x14 -> x2, local copies, waits for them, and re-layouts: 5.92 us -> 0.01 us
    pallas_call x1, Pallas kernels: 37.1 us -> 34.1 us  [shards(): pl.pallas_call(solve_kernel, out_shape=jax.ShapeDtypeStruct((CAP, SPINS,...]
where the time goes in v4:
time: 36.7 us; the launch traced here: 36.6 us
  Pallas kernels  36.6 us (100%)
    pallas_call x1, Pallas kernels, shards(): pl.pallas_call(solve_kernel, out_shape=jax.ShapeDtypeStruct((CAP, SPINS,...  34.1 us
    pallas_call x1, Pallas kernels, shards(): pl.pallas_call(assemble_kernel, out_shape=jax.ShapeDtypeStruct((CAP, SPIN...  2.47 us

profile of v4, /device:TPU:96, one launch (start us, length us, event | category | flops | bytes accessed | tf_op | source)
XLA Modules:
  0.0 36.6 jit_solution(3556080548087638896)
XLA Ops:
  0.0 0.0 copy-start
  0.0 34.1 %shard_map.82.ready = f32[7,2,64000]{2,1,0:T(2,128)S(1)} custom-call(s32[512]{0:T(512)} %dest.1, s32[2,512]{1,0:T(2,128)} %bitcast.4, s32[3,512]{1,0:T(4,128)} %bitcast.3, bf16[2,4,64000]{2,1,0:T(4,128)(2,1)} %orbitals_hbm.1, bf16[160,160]{1,0:T(8,128)(2,1)} %constant.8.clone.first_hbm, bf16[1664,1664]{1,0:T(8,128)(2,1)} %constant.9.clone.both_hbm, ...), custom_call_target="tpu_custom_call" | custom-call | tf_op jit(solution)/shard_map/pallas_call | solution.py:446
  34.1 0.0 copy-done
  34.1 2.5 %shard_map.83 = f32[7,2,64000]{2,1,0:T(2,128)} custom-call(s32[512]{0:T(512)S(1)} %copy-done, f32[7,2,64000]{2,1,0:T(2,128)S(1)} %shard_map.82.ready), custom_call_target="tpu_custom_call" | custom-call | tf_op jit(solution)/shard_map/pallas_call | solution.py:480
Async XLA Ops:
  0.0 34.1 %copy-start = (s32[512]{0:T(512)S(1)}, s32[512]{0:T(512)}, u32[]{:S(2)}) copy-start(s32[512]{0:T(512)} %dest.1) | copy-start | bytes 6148

commit v5 on v4

--- a/solution.py
+++ b/solution.py
@@ -24,6 +24,8 @@
 LANE = 128
 TILES = 13
 WIDTH = TILES * LANE
+FOLDED = TILES // 2
+HALF = (FOLDED + 1) * LANE
 OFF = (WIDTH - PLANE) // 2
 MARGIN = 7 * LANE
 WIDE = WIDTH + 2 * MARGIN
@@ -47,9 +49,19 @@
     inverse = np.concatenate([inverse, inverse], axis=0)
     sine32 = sine.astype(np.float32)
     first = np.kron(np.eye(4, dtype=np.float32), sine32).astype(ml_dtypes.bfloat16)
-    both = np.zeros((WIDTH, WIDTH), np.float32)
-    both[OFF : OFF + PLANE, OFF : OFF + PLANE] = np.kron(sine32, sine32)
-    both = both.astype(ml_dtypes.bfloat16)
+    plane_sine = np.zeros((WIDTH, PLANE), np.float32)
+    plane_sine[OFF : OFF + PLANE] = np.kron(sine32, sine32)
+    mode = np.arange(PLANE)
+    odd = (mode // EDGE + mode % EDGE) % 2
+    both = np.zeros((2, 2, HALF, HALF), np.float32)
+    scale = np.zeros((2 * EDGE, 2 * HALF), np.float32)
+    for parity in range(2):
+        chosen = mode[odd == parity]
+        both[parity, 0, :, : chosen.size] = plane_sine[:HALF, chosen]
+        both[parity, 1] = both[parity, 0].T
+        scale[:, parity * HALF : parity * HALF + chosen.size] = inverse[:, OFF + chosen]
+    inverse = scale
+    both = both.reshape(4 * HALF, HALF).astype(ml_dtypes.bfloat16)
     cells = np.full((2, WIDTH), -1000, np.int32)
     cells[0, OFF : OFF + PLANE] = np.arange(PLANE) // EDGE
     cells[1, OFF : OFF + PLANE] = np.arange(PLANE) % EDGE
@@ -194,32 +206,51 @@
         density[pair_row : pair_row + ROWS, span] = product.astype(jnp.bfloat16)
 
 
-def by_chunk(body):
-    for start in range(0, WIDTH, 256):
-        body(start, min(256, WIDTH - start))
-
-
-def solve(density, work, first, both, inverse, low, rows):
-    span = slice(low, low + rows)
-    for block in range(rows // (2 * ROWS)):
-        part = slice(low + block * 2 * ROWS, low + (block + 1) * 2 * ROWS)
-        work[part, :] = jnp.dot(
-            first[...], density[part, :], preferred_element_type=jnp.float32
-        ).astype(jnp.bfloat16)
-
-    def forward(start, size):
-        cut = pl.ds(start, size)
-        out = jnp.dot(work[span, :], both[:, cut], preferred_element_type=jnp.float32)
-        out = out.reshape(rows // ROWS, ROWS, size) * inverse[:, cut][None]
-        density[span, cut] = out.reshape(rows, size).astype(jnp.bfloat16)
-
-    def backward(start, size):
-        cut = pl.ds(start, size)
-        out = jnp.dot(density[span, :], both[:, cut], preferred_element_type=jnp.float32)
-        work[span, cut] = out.astype(jnp.bfloat16)
-
-    by_chunk(forward)
-    by_chunk(backward)
+def mirrored(value):
+    lanes = LANE - 1 - lax.broadcasted_iota(jnp.int32, value.shape, 1)
+    return jnp.take_along_axis(value, lanes, axis=1)
+
+
+def tile_of(value, tile):
+    return value[:, tile * LANE : (tile + 1) * LANE]
+
+
+def solve(density, work, folded, modes, first, both, inverse, low):
+    rows = slice(low, low + 2 * ROWS)
+    value = jnp.dot(first[...], density[rows, :], preferred_element_type=jnp.float32)
+    for tile in range(FOLDED):
+        here = tile_of(value, tile)
+        there = mirrored(tile_of(value, TILES - 1 - tile))
+        span = slice(tile * LANE, (tile + 1) * LANE)
+        folded[0, rows, span] = (here + there).astype(jnp.bfloat16)
+        folded[1, rows, span] = (here - there).astype(jnp.bfloat16)
+    middle = tile_of(value, FOLDED).astype(jnp.bfloat16)
+    for parity in range(2):
+        folded[parity, rows, FOLDED * LANE :] = middle
+    for parity in range(2):
+        for start in range(0, HALF, 256):
+            stop = min(start + 256, HALF)
+            table = both[2 * parity * HALF : (2 * parity + 1) * HALF, start:stop]
+            out = jnp.dot(folded[parity, rows, :], table, preferred_element_type=jnp.float32)
+            scale = inverse[:, parity * HALF + start : parity * HALF + stop]
+            out = out * jnp.concatenate([scale, scale], axis=0)
+            modes[parity, rows, start:stop] = out.astype(jnp.bfloat16)
+    for start in range(0, HALF, 256):
+        stop = min(start + 256, HALF)
+        even, odd = (
+            jnp.dot(
+                modes[parity, rows, :],
+                both[(2 * parity + 1) * HALF : (2 * parity + 2) * HALF, start:stop],
+                preferred_element_type=jnp.float32,
+            )
+            for parity in range(2)
+        )
+        work[rows, start:stop] = (even + odd).astype(jnp.bfloat16)
+        for tile in range(start // LANE, min(stop // LANE, FOLDED)):
+            inside = slice(tile * LANE - start, (tile + 1) * LANE - start)
+            mirror = mirrored(even[:, inside] - odd[:, inside]).astype(jnp.bfloat16)
+            target = TILES - 1 - tile
+            work[rows, target * LANE : (target + 1) * LANE] = mirror
 
 
 def flatten_rows(lines, place):
@@ -266,7 +297,7 @@
     dest_hbm, partners_hbm, anchors_hbm, orbitals_hbm, first_hbm, both_hbm, inverse_hbm, cells_hbm,
     ready,
     dest, partners, anchors, orbitals, first, inverse, cells,
-    boxes, moved, density, work, both, lines, flat, box_out, box_in, sends, arrived,
+    boxes, moved, density, work, folded, modes, both, lines, flat, box_out, box_in, sends, arrived,
     load_sems, box_send, box_recv, move_send, move_recv,
 ):
     device = device_number()
@@ -373,7 +404,7 @@
     for spot in range(BOX_DEV):
         if spot + 1 < BOX_DEV:
             shift_box(spot + 1)
-        solve(density, work, first, both, inverse, spot * 2 * ROWS, 2 * ROWS)
+        solve(density, work, folded, modes, first, both, inverse, spot * 2 * ROWS)
         span = slice(spot * 2 * ROWS, (spot + 1) * 2 * ROWS)
         potential = jnp.dot(first[...], work[span, :], preferred_element_type=jnp.float32)
         terms = potential * moved[span, :]
@@ -433,7 +464,7 @@
         pltpu.make_async_copy(blank, out.at[slot], sems.at[slot]).wait()
 
 
-VMEM_LIMIT = 36 * 1024 * 1024
+VMEM_LIMIT = 42 * 1024 * 1024
 
 
 def shards(orbitals, dest, partners, anchors):
@@ -460,7 +491,9 @@
             pltpu.VMEM((PAIR_ROWS, WIDTH), jnp.float32),
             pltpu.VMEM((PAIR_ROWS, WIDTH), jnp.bfloat16),
             pltpu.VMEM((PAIR_ROWS, WIDTH), jnp.bfloat16),
-            pltpu.VMEM((WIDTH, WIDTH), jnp.bfloat16),
+            pltpu.VMEM((2, PAIR_ROWS, HALF), jnp.bfloat16),
+            pltpu.VMEM((2, PAIR_ROWS, HALF), jnp.bfloat16),
+            pltpu.VMEM(both.shape, both.dtype),
             pltpu.VMEM((TILES, BOX_DEV * ROWS, LANE), jnp.float32),
             pltpu.VMEM((BOX_DEV, OUT_ROWS, LANE), jnp.float32),
             pltpu.VMEM((2, TILES, ROWS, LANE), jnp.bfloat16),

time: 36.7 us -> 35.3 us (0.962)
  Pallas kernels: 36.6 us -> 35.2 us
    pallas_call x1, Pallas kernels: 34.1 us -> 32.7 us  [shards(): pl.pallas_call(solve_kernel, out_shape=jax.ShapeDtypeStruct((CAP, SPINS,...]
where the time goes in v5:
time: 35.3 us; the launch traced here: 35.2 us
  Pallas kernels  35.2 us (100%)
    pallas_call x1, Pallas kernels, shards(): pl.pallas_call(solve_kernel, out_shape=jax.ShapeDtypeStruct((CAP, SPINS,...  32.7 us
    pallas_call x1, Pallas kernels, shards(): pl.pallas_call(assemble_kernel, out_shape=jax.ShapeDtypeStruct((CAP, SPIN...  2.47 us

profile of v5, /device:TPU:96, one launch (start us, length us, event | category | flops | bytes accessed | tf_op | source)
XLA Modules:
  0.0 35.2 jit_solution(12363020623933495535)
XLA Ops:
  0.0 0.0 copy-start
  0.0 32.7 %shard_map.82.ready = f32[7,2,64000]{2,1,0:T(2,128)S(1)} custom-call(s32[512]{0:T(512)} %dest.1, s32[2,512]{1,0:T(2,128)} %bitcast.4, s32[3,512]{1,0:T(4,128)} %bitcast.3, bf16[2,4,64000]{2,1,0:T(4,128)(2,1)} %orbitals_hbm.1, bf16[160,160]{1,0:T(8,128)(2,1)} %constant.8.clone.first_hbm, bf16[3584,896]{1,0:T(8,128)(2,1)} %constant.9.clone.both_hbm, ...), custom_call_target="tpu_custom_call" | custom-call | tf_op jit(solution)/shard_map/pallas_call | solution.py:477
  32.7 0.0 copy-done
  32.7 2.5 %shard_map.83 = f32[7,2,64000]{2,1,0:T(2,128)} custom-call(s32[512]{0:T(512)S(1)} %copy-done, f32[7,2,64000]{2,1,0:T(2,128)S(1)} %shard_map.82.ready), custom_call_target="tpu_custom_call" | custom-call | tf_op jit(solution)/shard_map/pallas_call | solution.py:513
Async XLA Ops:
  0.0 32.7 %copy-start = (s32[512]{0:T(512)S(1)}, s32[512]{0:T(512)}, u32[]{:S(2)}) copy-start(s32[512]{0:T(512)} %dest.1) | copy-start | bytes 6148

commit v6 on v5

--- a/solution.py
+++ b/solution.py
@@ -33,6 +33,7 @@
 PAIR_ROWS = BOX_DEV * 2 * ROWS
 OUT_ROWS = SPINS * CELLS // LANE
 GROUP = 25
+TURNS = (0, 2, 1, 3)
 EMPTY = MARGIN // LANE
 SPREAD = WIDE // LANE
 MESH = pl.DeviceIdType.MESH
@@ -157,21 +158,23 @@
     return chosen
 
 
-def unpack_rows(orbitals, lines, boxes):
+def unpack_rows(spin, orbitals, lines):
     def pair(number, carry):
         start = pl.multiple_of(number * 2 * PLANE, LANE)
-        for spin in range(SPINS):
-            cells = orbitals[spin, :, pl.ds(start, 2 * PLANE)].astype(jnp.float32)
-            even = pltpu.roll(cells[:, :WIDTH], OFF, 1)
-            odd = pltpu.roll(cells[:, 2 * PLANE - WIDTH :], WIDTH - OFF, 1)
-            row = spin * EDGE + 2 * number
-            for tile in range(TILES):
-                span = slice(tile * LANE, (tile + 1) * LANE)
-                lines[tile, pl.ds(row, BOX_DEV, stride=ROWS), :] = even[:, span]
-                lines[tile, pl.ds(row + 1, BOX_DEV, stride=ROWS), :] = odd[:, span]
+        cells = orbitals[spin, :, pl.ds(start, 2 * PLANE)].astype(jnp.float32)
+        even = pltpu.roll(cells[:, :WIDTH], OFF, 1)
+        odd = pltpu.roll(cells[:, 2 * PLANE - WIDTH :], WIDTH - OFF, 1)
+        row = spin * EDGE + 2 * number
+        for tile in range(TILES):
+            span = slice(tile * LANE, (tile + 1) * LANE)
+            lines[tile, pl.ds(row, BOX_DEV, stride=ROWS), :] = even[:, span]
+            lines[tile, pl.ds(row + 1, BOX_DEV, stride=ROWS), :] = odd[:, span]
         return carry
 
     lax.fori_loop(0, EDGE // 2, pair, 0, unroll=4)
+
+
+def gather_tiles(lines, boxes):
     for box in range(BOX_DEV):
         for tile in range(TILES):
             value = lines[tile, box * ROWS : (box + 1) * ROWS, :]
@@ -319,7 +322,8 @@
         pltpu.make_async_copy(source, target, load_sems.at[number])
         for number, (source, target) in enumerate(
             (
-                (orbitals_hbm, orbitals),
+                (orbitals_hbm.at[0], orbitals.at[0]),
+                (orbitals_hbm.at[1], orbitals.at[1]),
                 (dest_hbm, dest),
                 (partners_hbm, partners),
                 (anchors_hbm, anchors),
@@ -330,7 +334,7 @@
             )
         )
     ]
-    for load in loads:
+    for load in loads[:5]:
         load.start()
 
     def box_copy(way):
@@ -352,9 +356,13 @@
         for tile in range(EMPTY):
             boxes[box * SPREAD + tile] = blank
             boxes[box * SPREAD + EMPTY + TILES + tile] = blank
-    loads[0].wait()
-    unpack_rows(orbitals, lines, boxes)
-    for load in loads[1:4]:
+    for spin in range(SPINS):
+        loads[spin].wait()
+        unpack_rows(spin, orbitals, lines)
+    for load in loads[5:]:
+        load.start()
+    gather_tiles(lines, boxes)
+    for load in loads[2:5]:
         load.wait()
     for way, other in enumerate((device + 1, device - 1)):
         chosen = shared_box(partners, device, other)
@@ -398,12 +406,12 @@
             row = (spot * 2 + which) * ROWS
             shift_pair(boxes, moved, density, cells, order[spot], place, delta, row)
 
-    for load in loads[4:]:
+    for load in loads[5:]:
         load.wait()
-    shift_box(0)
-    for spot in range(BOX_DEV):
-        if spot + 1 < BOX_DEV:
-            shift_box(spot + 1)
+    shift_box(TURNS[0])
+    for turn, spot in enumerate(TURNS):
+        if turn + 1 < BOX_DEV:
+            shift_box(TURNS[turn + 1])
         solve(density, work, folded, modes, first, both, inverse, spot * 2 * ROWS)
         span = slice(spot * 2 * ROWS, (spot + 1) * 2 * ROWS)
         potential = jnp.dot(first[...], work[span, :], preferred_element_type=jnp.float32)
@@ -500,7 +508,7 @@
             pltpu.VMEM((2, TILES, ROWS, LANE), jnp.bfloat16),
             pltpu.VMEM((3, OUT_ROWS, LANE), jnp.bfloat16),
             pltpu.VMEM((3, OUT_ROWS, LANE), jnp.bfloat16),
-            pltpu.SemaphoreType.DMA((8,)),
+            pltpu.SemaphoreType.DMA((9,)),
             pltpu.SemaphoreType.DMA((2,)),
             pltpu.SemaphoreType.DMA((2,)),
             pltpu.SemaphoreType.DMA((3,)),

time: 35.3 us -> 33.1 us (0.938)
  Pallas kernels: 35.2 us -> 32.8 us
    pallas_call x1, Pallas kernels: 32.7 us -> 30.3 us  [shards(): pl.pallas_call(solve_kernel, out_shape=jax.ShapeDtypeStruct((CAP, SPINS,...]
where the time goes in v6:
time: 33.1 us; the launch traced here: 32.8 us
  Pallas kernels  32.8 us (99%)
    pallas_call x1, Pallas kernels, shards(): pl.pallas_call(solve_kernel, out_shape=jax.ShapeDtypeStruct((CAP, SPINS,...  30.3 us
    pallas_call x1, Pallas kernels, shards(): pl.pallas_call(assemble_kernel, out_shape=jax.ShapeDtypeStruct((CAP, SPIN...  2.47 us

profile of v6, /device:TPU:96, one launch (start us, length us, event | category | flops | bytes accessed | tf_op | source)
XLA Modules:
  0.0 32.8 jit_solution(10362219982193624778)
XLA Ops:
  0.0 0.0 copy-start
  0.0 30.3 %shard_map.82.ready = f32[7,2,64000]{2,1,0:T(2,128)S(1)} custom-call(s32[512]{0:T(512)} %dest.1, s32[2,512]{1,0:T(2,128)} %bitcast.4, s32[3,512]{1,0:T(4,128)} %bitcast.3, bf16[2,4,64000]{2,1,0:T(4,128)(2,1)} %orbitals_hbm.1, bf16[160,160]{1,0:T(8,128)(2,1)} %constant.8.clone.first_hbm, bf16[3584,896]{1,0:T(8,128)(2,1)} %constant.9.clone.both_hbm, ...), custom_call_target="tpu_custom_call" | custom-call | tf_op jit(solution)/shard_map/pallas_call | solution.py:485
  30.3 0.0 copy-done
  30.3 2.5 %shard_map.83 = f32[7,2,64000]{2,1,0:T(2,128)} custom-call(s32[512]{0:T(512)S(1)} %copy-done, f32[7,2,64000]{2,1,0:T(2,128)S(1)} %shard_map.82.ready), custom_call_target="tpu_custom_call" | custom-call | tf_op jit(solution)/shard_map/pallas_call | solution.py:521
Async XLA Ops:
  0.0 30.3 %copy-start = (s32[512]{0:T(512)S(1)}, s32[512]{0:T(512)}, u32[]{:S(2)}) copy-start(s32[512]{0:T(512)} %dest.1) | copy-start | bytes 6148

commit v7 on v5

--- a/solution.py
+++ b/solution.py
@@ -33,9 +33,18 @@
 PAIR_ROWS = BOX_DEV * 2 * ROWS
 OUT_ROWS = SPINS * CELLS // LANE
 GROUP = 25
+EARLY = 24
+PARTS = ((0, EARLY), (EARLY, EDGE))
+SPLIT = SPINS * EARLY
+TURNS = (0, 2, 1, 3)
 EMPTY = MARGIN // LANE
 SPREAD = WIDE // LANE
 MESH = pl.DeviceIdType.MESH
+
+
+def row_order():
+    pairs = [(spin, a) for low, high in PARTS for spin in range(SPINS) for a in range(low, high)]
+    return tuple(np.array(column) for column in zip(*pairs))
 
 
 def tables():
@@ -46,9 +55,13 @@
     plane = (levels[:, None] + levels[None, :]).reshape(-1)
     inverse = np.zeros((EDGE, WIDTH), np.float32)
     inverse[:, OFF : OFF + PLANE] = 1.0 / (levels[:, None] + plane[None, :] + SCREEN)
-    inverse = np.concatenate([inverse, inverse], axis=0)
+    spins, planes = row_order()
+    inverse = inverse[planes]
     sine32 = sine.astype(np.float32)
-    first = np.kron(np.eye(4, dtype=np.float32), sine32).astype(ml_dtypes.bfloat16)
+    first = sine32[planes][:, planes] * (spins[:, None] == spins[None, :])
+    first = np.kron(np.eye(2, dtype=np.float32), first).astype(ml_dtypes.bfloat16)
+    steps = np.where(spins[:, None] == spins[None, :], planes[None, :] - planes[:, None], 1000)
+    steps = steps.astype(np.int32)
     plane_sine = np.zeros((WIDTH, PLANE), np.float32)
     plane_sine[OFF : OFF + PLANE] = np.kron(sine32, sine32)
     mode = np.arange(PLANE)
@@ -65,7 +78,7 @@
     cells = np.full((2, WIDTH), -1000, np.int32)
     cells[0, OFF : OFF + PLANE] = np.arange(PLANE) // EDGE
     cells[1, OFF : OFF + PLANE] = np.arange(PLANE) % EDGE
-    return first, both, inverse, cells
+    return first, both, inverse, cells, steps
 
 
 def device_number():
@@ -157,36 +170,36 @@
     return chosen
 
 
-def unpack_rows(orbitals, lines, boxes):
+def unpack_rows(part, orbitals, lines, boxes):
+    low, high = PARTS[part]
+
     def pair(number, carry):
         start = pl.multiple_of(number * 2 * PLANE, LANE)
         for spin in range(SPINS):
             cells = orbitals[spin, :, pl.ds(start, 2 * PLANE)].astype(jnp.float32)
             even = pltpu.roll(cells[:, :WIDTH], OFF, 1)
             odd = pltpu.roll(cells[:, 2 * PLANE - WIDTH :], WIDTH - OFF, 1)
-            row = spin * EDGE + 2 * number
+            row = part * SPLIT + spin * (high - low) + 2 * number - low
             for tile in range(TILES):
                 span = slice(tile * LANE, (tile + 1) * LANE)
                 lines[tile, pl.ds(row, BOX_DEV, stride=ROWS), :] = even[:, span]
                 lines[tile, pl.ds(row + 1, BOX_DEV, stride=ROWS), :] = odd[:, span]
         return carry
 
-    lax.fori_loop(0, EDGE // 2, pair, 0, unroll=4)
+    lax.fori_loop(low // 2, high // 2, pair, 0, unroll=4)
+    rows = slice(part * SPLIT, SPLIT if part == 0 else ROWS)
     for box in range(BOX_DEV):
         for tile in range(TILES):
-            value = lines[tile, box * ROWS : (box + 1) * ROWS, :]
-            boxes[box * SPREAD + EMPTY + tile] = value.astype(jnp.bfloat16)
-
-
-def shift_pair(boxes, moved, density, cells, center, partner, delta, pair_row):
+            value = lines[tile, box * ROWS + rows.start : box * ROWS + rows.stop, :]
+            boxes[box * SPREAD + EMPTY + tile, rows, :] = value.astype(jnp.bfloat16)
+
+
+def shift_pair(boxes, moved, density, cells, steps, center, partner, delta, pair_row):
     flat = MARGIN - (delta[1] * EDGE + delta[2])
     column = flat // LANE
     turn = flat - column * LANE
     keep = lax.broadcasted_iota(jnp.int32, (ROWS, LANE), 1) < LANE - turn
-    row = lax.broadcasted_iota(jnp.int32, (ROWS, ROWS), 0)
-    source = lax.broadcasted_iota(jnp.int32, (ROWS, ROWS), 1)
-    same = (row >= EDGE) == (source >= EDGE)
-    shifter = (same & (source == row - delta[0])).astype(jnp.float32).astype(jnp.bfloat16)
+    shifter = (steps[...] == -delta[0]).astype(jnp.float32).astype(jnp.bfloat16)
     first_tile = partner * SPREAD + column
     wide = jnp.concatenate([boxes[first_tile + tile] for tile in range(TILES + 1)], axis=1)
     wide = jnp.dot(shifter, wide, preferred_element_type=jnp.float32)
@@ -295,9 +308,10 @@
 
 def solve_kernel(
     dest_hbm, partners_hbm, anchors_hbm, orbitals_hbm, first_hbm, both_hbm, inverse_hbm, cells_hbm,
+    steps_hbm,
     ready,
-    dest, partners, anchors, orbitals, first, inverse, cells,
-    boxes, moved, density, work, folded, modes, both, lines, flat, box_out, box_in, sends, arrived,
+    dest, partners, anchors, orbitals, first, inverse, cells, steps,
+    boxes, moved, density, work, folded, modes, both, lines, flat, early_out, late_out, early_in, late_in, sends, arrived,
     load_sems, box_send, box_recv, move_send, move_recv,
 ):
     device = device_number()
@@ -319,24 +333,29 @@
         pltpu.make_async_copy(source, target, load_sems.at[number])
         for number, (source, target) in enumerate(
             (
-                (orbitals_hbm, orbitals),
+                (orbitals_hbm.at[:, :, : EARLY * PLANE], orbitals.at[:, :, : EARLY * PLANE]),
+                (orbitals_hbm.at[:, :, EARLY * PLANE :], orbitals.at[:, :, EARLY * PLANE :]),
                 (dest_hbm, dest),
                 (partners_hbm, partners),
                 (anchors_hbm, anchors),
                 (first_hbm, first),
                 (cells_hbm, cells),
+                (steps_hbm, steps),
                 (inverse_hbm, inverse),
                 (both_hbm, both),
             )
         )
     ]
-    for load in loads:
+    for load in loads[:5]:
         load.start()
 
-    def box_copy(way):
+    box_out = (early_out, late_out)
+    box_in = (early_in, late_in)
+
+    def box_copy(way, part):
         return pltpu.make_async_remote_copy(
-            src_ref=box_out.at[way], dst_ref=box_in.at[way],
-            send_sem=box_send.at[way], recv_sem=box_recv.at[way],
+            src_ref=box_out[part].at[way], dst_ref=box_in[part].at[way],
+            send_sem=box_send.at[2 * part + way], recv_sem=box_recv.at[2 * part + way],
             device_id=(following, previous)[way], device_id_type=MESH,
         )
 
@@ -352,39 +371,42 @@
         for tile in range(EMPTY):
             boxes[box * SPREAD + tile] = blank
             boxes[box * SPREAD + EMPTY + TILES + tile] = blank
-    loads[0].wait()
-    unpack_rows(orbitals, lines, boxes)
-    for load in loads[1:4]:
-        load.wait()
-    for way, other in enumerate((device + 1, device - 1)):
-        chosen = shared_box(partners, device, other)
-        for tile in range(TILES):
-            box_out[way, tile] = boxes[chosen * SPREAD + EMPTY + tile]
-
-    pl.semaphore_wait(barrier, has_next.astype(jnp.int32) + has_prev.astype(jnp.int32))
-
-    @pl.when(has_next)
-    def _():
-        box_copy(0).start()
-
-    @pl.when(has_prev)
-    def _():
-        box_copy(1).start()
+    for part in range(2):
+        rows = slice(part * SPLIT, SPLIT if part == 0 else ROWS)
+        loads[part].wait()
+        unpack_rows(part, orbitals, lines, boxes)
+        if part == 0:
+            for load in loads[2:5]:
+                load.wait()
+            for load in loads[5:]:
+                load.start()
+            chosen = [shared_box(partners, device, other) for other in (device + 1, device - 1)]
+        for way in range(2):
+            for tile in range(TILES):
+                box_out[part][way, tile] = boxes[chosen[way] * SPREAD + EMPTY + tile][rows, :]
+        if part == 0:
+            pl.semaphore_wait(barrier, has_next.astype(jnp.int32) + has_prev.astype(jnp.int32))
+
+        @pl.when(has_next)
+        def _():
+            box_copy(0, part).start()
+
+        @pl.when(has_prev)
+        def _():
+            box_copy(1, part).start()
 
     order = boxes_by_position(dest, device)
     base = device * BOX_DEV
-
-    @pl.when(has_prev)
-    def _():
-        box_copy(0).wait_recv()
-        for tile in range(TILES):
-            boxes[BOX_DEV * SPREAD + EMPTY + tile] = box_in[0, tile]
-
-    @pl.when(has_next)
-    def _():
-        box_copy(1).wait_recv()
-        for tile in range(TILES):
-            boxes[(BOX_DEV + 1) * SPREAD + EMPTY + tile] = box_in[1, tile]
+    for way, comes in ((0, has_prev), (1, has_next)):
+
+        @pl.when(comes)
+        def _():
+            for part in range(2):
+                rows = slice(part * SPLIT, SPLIT if part == 0 else ROWS)
+                box_copy(way, part).wait_recv()
+                for tile in range(TILES):
+                    place = (BOX_DEV + way) * SPREAD + EMPTY + tile
+                    boxes[place, rows, :] = box_in[part][way, tile]
 
     def shift_box(spot):
         box = base + order[spot]
@@ -396,21 +418,26 @@
                 wrapped(anchors[dim, partner] - anchors[dim, box], GRID[dim]) for dim in range(3)
             ]
             row = (spot * 2 + which) * ROWS
-            shift_pair(boxes, moved, density, cells, order[spot], place, delta, row)
-
-    for load in loads[4:]:
+            shift_pair(boxes, moved, density, cells, steps, order[spot], place, delta, row)
+
+    for load in loads[5:]:
         load.wait()
-    shift_box(0)
-    for spot in range(BOX_DEV):
-        if spot + 1 < BOX_DEV:
-            shift_box(spot + 1)
+    shift_box(TURNS[0])
+    for turn, spot in enumerate(TURNS):
+        if turn + 1 < BOX_DEV:
+            shift_box(TURNS[turn + 1])
         solve(density, work, folded, modes, first, both, inverse, spot * 2 * ROWS)
         span = slice(spot * 2 * ROWS, (spot + 1) * 2 * ROWS)
         potential = jnp.dot(first[...], work[span, :], preferred_element_type=jnp.float32)
         terms = potential * moved[span, :]
         total = terms[:ROWS] + terms[ROWS:]
         for tile in range(TILES):
-            lines[tile, :ROWS, :] = total[:, tile * LANE : (tile + 1) * LANE]
+            row = 0
+            for low, high in PARTS:
+                for spin in range(SPINS):
+                    piece = total[row : row + high - low, tile * LANE : (tile + 1) * LANE]
+                    lines[tile, spin * EDGE + low : spin * EDGE + high, :] = piece
+                    row += high - low
 
         def place(row, value):
             flat[spot, pl.ds(row, EDGE // 2, stride=2 * (2 * TILES - 1)), :] = value
@@ -436,12 +463,14 @@
 
     @pl.when(has_next)
     def _():
-        box_copy(0).wait_send()
+        box_copy(0, 0).wait_send()
+        box_copy(0, 1).wait_send()
         move_copy(2).wait_send()
 
     @pl.when(has_prev)
     def _():
-        box_copy(1).wait_send()
+        box_copy(1, 0).wait_send()
+        box_copy(1, 1).wait_send()
         move_copy(0).wait_send()
         move_copy(1).wait_send()
 
@@ -468,8 +497,8 @@
 
 
 def shards(orbitals, dest, partners, anchors):
-    first, both, inverse, cells = (jnp.asarray(table) for table in tables())
-    operands = (dest, partners.T, anchors.T, orbitals, first, both, inverse, cells)
+    first, both, inverse, cells, steps = (jnp.asarray(table) for table in tables())
+    operands = (dest, partners.T, anchors.T, orbitals, first, both, inverse, cells, steps)
     operands = [pltpu.with_memory_space_constraint(operand, pltpu.HBM) for operand in operands]
     smem = pl.BlockSpec(memory_space=pltpu.SMEM)
     vmem = pl.BlockSpec(memory_space=pltpu.VMEM)
@@ -477,7 +506,7 @@
     ready = pl.pallas_call(
         solve_kernel,
         out_shape=jax.ShapeDtypeStruct((CAP, SPINS, CELLS), jnp.float32),
-        in_specs=[pl.BlockSpec(memory_space=pltpu.HBM)] * 8,
+        in_specs=[pl.BlockSpec(memory_space=pltpu.HBM)] * 9,
         out_specs=vmem,
         scratch_shapes=[
             pltpu.SMEM((BOXES,), jnp.int32),
@@ -487,6 +516,7 @@
             pltpu.VMEM(first.shape, first.dtype),
             pltpu.VMEM(inverse.shape, inverse.dtype),
             pltpu.VMEM(cells.shape, cells.dtype),
+            pltpu.VMEM(steps.shape, steps.dtype),
             pltpu.VMEM(((BOX_DEV + 2) * SPREAD, ROWS, LANE), jnp.bfloat16),
             pltpu.VMEM((PAIR_ROWS, WIDTH), jnp.float32),
             pltpu.VMEM((PAIR_ROWS, WIDTH), jnp.bfloat16),
@@ -496,13 +526,15 @@
             pltpu.VMEM(both.shape, both.dtype),
             pltpu.VMEM((TILES, BOX_DEV * ROWS, LANE), jnp.float32),
             pltpu.VMEM((BOX_DEV, OUT_ROWS, LANE), jnp.float32),
-            pltpu.VMEM((2, TILES, ROWS, LANE), jnp.bfloat16),
-            pltpu.VMEM((2, TILES, ROWS, LANE), jnp.bfloat16),
+            pltpu.VMEM((2, TILES, SPLIT, LANE), jnp.bfloat16),
+            pltpu.VMEM((2, TILES, ROWS - SPLIT, LANE), jnp.bfloat16),
+            pltpu.VMEM((2, TILES, SPLIT, LANE), jnp.bfloat16),
+            pltpu.VMEM((2, TILES, ROWS - SPLIT, LANE), jnp.bfloat16),
             pltpu.VMEM((3, OUT_ROWS, LANE), jnp.bfloat16),
             pltpu.VMEM((3, OUT_ROWS, LANE), jnp.bfloat16),
-            pltpu.SemaphoreType.DMA((8,)),
-            pltpu.SemaphoreType.DMA((2,)),
-            pltpu.SemaphoreType.DMA((2,)),
+            pltpu.SemaphoreType.DMA((10,)),
+            pltpu.SemaphoreType.DMA((4,)),
+            pltpu.SemaphoreType.DMA((4,)),
             pltpu.SemaphoreType.DMA((3,)),
             pltpu.SemaphoreType.DMA((3,)),
         ],

time: 35.3 us -> 32.9 us (0.932)
  Pallas kernels: 35.2 us -> 32.8 us
    pallas_call x1, Pallas kernels: 32.7 us -> 30.3 us  [shards(): pl.pallas_call(solve_kernel, out_shape=jax.ShapeDtypeStruct((CAP, SPINS,...]
where the time goes in v7:
time: 32.9 us; the launch traced here: 32.8 us
  Pallas kernels  32.8 us (100%)
    pallas_call x1, Pallas kernels, shards(): pl.pallas_call(solve_kernel, out_shape=jax.ShapeDtypeStruct((CAP, SPINS,...  30.3 us
    pallas_call x1, Pallas kernels, shards(): pl.pallas_call(assemble_kernel, out_shape=jax.ShapeDtypeStruct((CAP, SPIN...  2.47 us

profile of v7, /device:TPU:96, one launch (start us, length us, event | category | flops | bytes accessed | tf_op | source)
XLA Modules:
  0.0 32.8 jit_solution(14194638669992598787)
XLA Ops:
  0.0 0.0 copy-start
  0.0 30.3 %shard_map.91.ready = f32[7,2,64000]{2,1,0:T(2,128)S(1)} custom-call(s32[512]{0:T(512)} %dest.1, s32[2,512]{1,0:T(2,128)} %bitcast.4, s32[3,512]{1,0:T(4,128)} %bitcast.3, bf16[2,4,64000]{2,1,0:T(4,128)(2,1)} %orbitals_hbm.1, bf16[160,160]{1,0:T(8,128)(2,1)} %constant.10.clone.first_hbm, bf16[3584,896]{1,0:T(8,128)(2,1)} %constant.11.clone.both_hbm, ...), custom_call_target="tpu_custom_call" | custom-call | tf_op jit(solution)/shard_map/pallas_call | solution.py:506
  30.3 0.0 copy-done
  30.3 2.5 %shard_map.92 = f32[7,2,64000]{2,1,0:T(2,128)} custom-call(s32[512]{0:T(512)S(1)} %copy-done, f32[7,2,64000]{2,1,0:T(2,128)S(1)} %shard_map.91.ready), custom_call_target="tpu_custom_call" | custom-call | tf_op jit(solution)/shard_map/pallas_call | solution.py:545
Async XLA Ops:
  0.0 30.3 %copy-start = (s32[512]{0:T(512)S(1)}, s32[512]{0:T(512)}, u32[]{:S(2)}) copy-start(s32[512]{0:T(512)} %dest.1) | copy-start | bytes 6148

commit v8 on v7

--- a/solution.py
+++ b/solution.py
@@ -33,7 +33,7 @@
 PAIR_ROWS = BOX_DEV * 2 * ROWS
 OUT_ROWS = SPINS * CELLS // LANE
 GROUP = 25
-EARLY = 24
+EARLY = 16
 PARTS = ((0, EARLY), (EARLY, EDGE))
 SPLIT = SPINS * EARLY
 TURNS = (0, 2, 1, 3)

time: 32.9 us -> 32.9 us (level)
  no operation moved by 1% of the time
where the time goes in v8:
time: 32.9 us; the launch traced here: 32.8 us
  Pallas kernels  32.8 us (100%)
    pallas_call x1, Pallas kernels, shards(): pl.pallas_call(solve_kernel, out_shape=jax.ShapeDtypeStruct((CAP, SPINS,...  30.3 us
    pallas_call x1, Pallas kernels, shards(): pl.pallas_call(assemble_kernel, out_shape=jax.ShapeDtypeStruct((CAP, SPIN...  2.47 us

profile of v8, /device:TPU:96, one launch (start us, length us, event | category | flops | bytes accessed | tf_op | source)
XLA Modules:
  0.0 32.8 jit_solution(9230456356701982378)
XLA Ops:
  0.0 0.0 copy-start
  0.0 30.3 %shard_map.91.ready = f32[7,2,64000]{2,1,0:T(2,128)S(1)} custom-call(s32[512]{0:T(512)} %dest.1, s32[2,512]{1,0:T(2,128)} %bitcast.4, s32[3,512]{1,0:T(4,128)} %bitcast.3, bf16[2,4,64000]{2,1,0:T(4,128)(2,1)} %orbitals_hbm.1, bf16[160,160]{1,0:T(8,128)(2,1)} %constant.10.clone.first_hbm, bf16[3584,896]{1,0:T(8,128)(2,1)} %constant.11.clone.both_hbm, ...), custom_call_target="tpu_custom_call" | custom-call | tf_op jit(solution)/shard_map/pallas_call | solution.py:506
  30.3 0.0 copy-done
  30.3 2.5 %shard_map.92 = f32[7,2,64000]{2,1,0:T(2,128)} custom-call(s32[512]{0:T(512)S(1)} %copy-done, f32[7,2,64000]{2,1,0:T(2,128)S(1)} %shard_map.91.ready), custom_call_target="tpu_custom_call" | custom-call | tf_op jit(solution)/shard_map/pallas_call | solution.py:545
Async XLA Ops:
  0.0 30.3 %copy-start = (s32[512]{0:T(512)S(1)}, s32[512]{0:T(512)}, u32[]{:S(2)}) copy-start(s32[512]{0:T(512)} %dest.1) | copy-start | bytes 6148
